TPU v7x, 32 devices: a whole 2x2x4 slice. The times are simulated.
32 devices in a mesh: row: 8 (over z, core), col: 4 (over y, x).
Axes of the slice: x: 2, y: 2, z: 4, core: 2. Of those that a mesh axis runs over, the one named last changes fastest.
Arguments:
- a_blocks: bfloat16 [8, 4, 96, 128, 128], P('row', 'col'), may hold values from -0.5 to 0.5
- a_rows: int32 [8, 4, 96], P('row', 'col'), may hold values from 0 to 7, as said below
- a_cols: int32 [8, 4, 96], P('row', 'col'), may hold values from 0 to 15, as said below
- p_blocks: bfloat16 [64, 128, 256], P(('row', 'col')), may hold values from -0.5 to 0.5
- coarse_slot: int32 [8, 4, 96, 4, 4], P('row', 'col'), may hold values from 0 to 31
Outputs:
- coarse_blocks: bfloat16 [8, 32, 4096], P('row', 'col')
Inputs may be any that keep to these rules, and one draw needn't show every extreme that they name: On each owner the pairs (a_rows, a_cols) of its 96 blocks are distinct. On each owner the pairs (a_rows, a_cols) of its 96 blocks are distinct.
All inputs are finite; a program needn't handle non-finite values.
Results may differ from a plain program's by a relative error of at most 0.0049.
Values may be sent and summed in bfloat16 or wider, within the bound.
No kernel may reach another device: no remote copies, remote signals or barrier semaphores. Data moves between devices by JAX's collectives and lax.ppermute only.
A program may use at most 128 MiB of HBM per device.

v0:
```python
import jax
import jax.numpy as jnp
from jax import lax
from jax.sharding import PartitionSpec as P

KS_DEV = 8


def owner_terms(blocks, row_ids, col_ids, slot_ids, row_panel, column_panel, slot_count):
    count = blocks.shape[0]
    group_size = 16
    groups = count // group_size
    node_width = blocks.shape[1]
    panel_width = row_panel.shape[2]
    agg_blocks = slot_ids.shape[1]
    agg_width = panel_width // agg_blocks

    def accumulate(running, batch_item):
        blk, rws, cls, sls = batch_item
        right_rows = jnp.take(column_panel, cls, axis=0)
        product = jnp.einsum(
            "kab,kbw->kaw", blk, right_rows, preferred_element_type=jnp.float32
        ).astype(jnp.bfloat16)
        left_rows = jnp.take(row_panel, rws, axis=0)
        left_split = left_rows.reshape(group_size, node_width, agg_blocks, agg_width)
        right_split = product.reshape(group_size, node_width, agg_blocks, agg_width)
        contribs = jnp.einsum(
            "knta,knsb->ktsab", left_split, right_split, preferred_element_type=jnp.float32
        )
        contribs = contribs.reshape(group_size * agg_blocks * agg_blocks, agg_width * agg_width)
        running = running.at[sls.reshape(-1)].add(contribs)
        return (running, None)

    items = (
        blocks.reshape(groups, group_size, node_width, node_width),
        row_ids.reshape(groups, group_size),
        col_ids.reshape(groups, group_size),
        slot_ids.reshape(groups, group_size, agg_blocks, agg_blocks),
    )
    start = jnp.zeros((slot_count, agg_width * agg_width), jnp.float32)
    running, _ = lax.scan(accumulate, start, items)
    return running


def on_device(a_blocks, a_rows, a_cols, p_blocks, coarse_slot):
    rows_total = lax.axis_size("row")
    cols_total = lax.axis_size("col")
    fan_count = rows_total // cols_total
    piece_rows = p_blocks.shape[0]
    tail_shape = p_blocks.shape[1:]
    row_panel = lax.all_gather(p_blocks, "col", axis=0, tiled=True)
    column_rows = lax.all_gather(p_blocks, "row", axis=0, tiled=True)
    grouped = column_rows.reshape((cols_total, fan_count, piece_rows) + tail_shape)
    regrouped = lax.all_to_all(grouped, "col", split_axis=0, concat_axis=2, tiled=True)
    column_panel = regrouped.reshape((fan_count * cols_total * piece_rows,) + tail_shape)
    slot_count = KS_DEV * cols_total
    running = owner_terms(
        a_blocks[0, 0],
        a_rows[0, 0],
        a_cols[0, 0],
        coarse_slot[0, 0],
        row_panel,
        column_panel,
        slot_count,
    )
    reduced = lax.psum_scatter(running, "col", scatter_dimension=0, tiled=True)
    return reduced.astype(jnp.bfloat16)[None]


def solution(mesh):
    placed = (
        P("row", "col", None, None, None),
        P("row", "col", None),
        P("row", "col", None),
        P(("row", "col"), None, None),
        P("row", "col", None, None, None),
    )
    return jax.shard_map(
        on_device, mesh=mesh, in_specs=placed, out_specs=P("row", "col", None), check_vma=False
    )
```

profile of v0, /device:TPU:0, one launch (start us, length us, event | category | flops | bytes accessed | tf_op | source)
XLA Modules:
  0.0 313.0 jit_solution(13129588461207719146)
XLA Ops:
  7.3 26.7 %all-gather.2.cloned.1.call-done = bf16[16,128,256]{2,1,0:T(8,128)(2,1)} async-done(((bf16[2,128,256]{2,1,0:T(8,128)(2,1)}), bf16[16,128,256]{2,1,0:T(8,128)(2,1)}) %all-gather.2.cloned.1.call-update) | async-done | bytes 1048592 | tf_op jit(solution)/shard_map/all_gather | solution.py:52
  33.9 3.7 %all-to-all-start = ((bf16[4,2,2,128,256]{4,3,2,1,0:T(8,128)(2,1)}), bf16[4,2,2,128,256]{4,3,2,1,0:T(8,128)(2,1)S(1)}, u32[]{:S(2)}, u32[]{:S(2)}) async-start(bf16[4,2,2,128,256]{4,3,2,1,0:T(8,128)(2,1)} %bitcast.67), calls=%async_computation | async-start | bytes 2097152 | tf_op jit(solution)/shard_map/all_to_all | solution.py:54
  38.2 1.4 reduce.6
  39.6 1.4 reduce.7
  41.9 1.3 dynamic-slice
  43.9 14.3 %all_gather.7 = bf16[8,128,256]{2,1,0:T(8,128)(2,1)S(1)} all-gather(bf16[2,128,256]{2,1,0:T(8,128)(2,1)} %param.10), channel_id=1, replica_groups=mesh['row'=8,'col'=4] {'col'}, dimensions={0}, use_global_device_ids=true | all-gather | bytes 655360 | tf_op jit(solution)/shard_map/all_gather | solution.py:51
  58.4 220.8 %while.10 = (s32[]{:T(128)}, f32[32,4096]{1,0:T(8,128)S(1)}, s32[6,16,4,4]{3,2,1,0:T(4,128)S(1)}, bf16[6,16,128,128]{3,2,1,0:T(8,128)(2,1)}, s32[6,16]{1,0:T(8,1...) while((s32[]{:T(128)}, f32[32,4096]{1,0:T(8,128)S(1)}, ...), condition=%wide.region_2.3_spmd, body=%wide.region_0.2_spmd.sunk | while | flops 405277728 | bytes 59261308 | solution.py:41
  59.4 1.5 convolution_convert_fusion.2
  60.9 1.3 copy.33
  62.9 1.4 copy.34
  64.3 5.8 %convolution_bitcast_fusion.2 = f32[16,4,4,64,64]{3,4,1,2,0:T(8,128)} fusion(bf16[16,128,4,64,1]{1,3,4,2,0:T(8,128)(2,1)S(1)} %bitcast.63, bf16[16,128,4,64]{1,3,2,0:T(8,128)(2,1)} %bitcast.64, pred[16]{0:T(512)(128)(4,1)S(1)} %get-tuple-element.156), kind=kOutput, calls=%fused_computation.3.clone.1 | convolution fusion | flops 268959744 | bytes 6291472 | tf_op jit(solution)/shard_map/while/body/eval_jaxpr/knta,knsb->ktsab/dot_general | solution.py:27
  70.0 9.3 %copy.35 = f32[16,4,4,64,64]{4,3,2,1,0:T(8,128)} copy(f32[16,4,4,64,64]{3,4,1,2,0:T(8,128)} %convolution_bitcast_fusion.2) | data formatting | bytes 8388608 | tf_op jit(solution)/shard_map/while/body/eval_jaxpr/knta,knsb->ktsab/transpose | solution.py:27
  79.3 7.9 %reshape.175 = f32[256,4096]{1,0:T(8,128)} reshape(f32[16,4,4,64,64]{4,3,2,1,0:T(8,128)} %copy.35) | data formatting | bytes 8388608 | tf_op jit(solution)/shard_map/while/body/eval_jaxpr/reshape | solution.py:30
  87.3 7.8 %scatter_fusion = f32[32,4096]{1,0:T(8,128)S(1)} fusion(f32[32,4096]{1,0:T(8,128)S(1)} %get-tuple-element.167, s32[256]{0:T(256)S(1)} %bitcast.69, f32[256,4096]{1,0:T(8,128)} %reshape.175), kind=kCustom, calls=%fused_computation.2.clone.1 | custom fusion | flops 1048576 | bytes 12583936 | tf_op jit(solution)/shard_map/while/body/eval_jaxpr/scatter-add | solution.py:31
  96.2 1.5 convolution_convert_fusion.2
  97.7 1.3 copy.33
  99.7 1.4 copy.34
  101.1 5.8 %convolution_bitcast_fusion.2 = f32[16,4,4,64,64]{3,4,1,2,0:T(8,128)} fusion(bf16[16,128,4,64,1]{1,3,4,2,0:T(8,128)(2,1)S(1)} %bitcast.63, bf16[16,128,4,64]{1,3,2,0:T(8,128)(2,1)} %bitcast.64, pred[16]{0:T(512)(128)(4,1)S(1)} %get-tuple-element.156), kind=kOutput, calls=%fused_computation.3.clone.1 | convolution fusion | flops 268959744 | bytes 6291472 | tf_op jit(solution)/shard_map/while/body/eval_jaxpr/knta,knsb->ktsab/dot_general | solution.py:27
  106.8 9.3 %copy.35 = f32[16,4,4,64,64]{4,3,2,1,0:T(8,128)} copy(f32[16,4,4,64,64]{3,4,1,2,0:T(8,128)} %convolution_bitcast_fusion.2) | data formatting | bytes 8388608 | tf_op jit(solution)/shard_map/while/body/eval_jaxpr/knta,knsb->ktsab/transpose | solution.py:27
  116.1 7.9 %reshape.175 = f32[256,4096]{1,0:T(8,128)} reshape(f32[16,4,4,64,64]{4,3,2,1,0:T(8,128)} %copy.35) | data formatting | bytes 8388608 | tf_op jit(solution)/shard_map/while/body/eval_jaxpr/reshape | solution.py:30
  124.1 7.8 %scatter_fusion = f32[32,4096]{1,0:T(8,128)S(1)} fusion(f32[32,4096]{1,0:T(8,128)S(1)} %get-tuple-element.167, s32[256]{0:T(256)S(1)} %bitcast.69, f32[256,4096]{1,0:T(8,128)} %reshape.175), kind=kCustom, calls=%fused_computation.2.clone.1 | custom fusion | flops 1048576 | bytes 12583936 | tf_op jit(solution)/shard_map/while/body/eval_jaxpr/scatter-add | solution.py:31
  133.0 1.5 convolution_convert_fusion.2
  134.5 1.3 copy.33
  136.5 1.4 copy.34
  137.8 5.8 %convolution_bitcast_fusion.2 = f32[16,4,4,64,64]{3,4,1,2,0:T(8,128)} fusion(bf16[16,128,4,64,1]{1,3,4,2,0:T(8,128)(2,1)S(1)} %bitcast.63, bf16[16,128,4,64]{1,3,2,0:T(8,128)(2,1)} %bitcast.64, pred[16]{0:T(512)(128)(4,1)S(1)} %get-tuple-element.156), kind=kOutput, calls=%fused_computation.3.clone.1 | convolution fusion | flops 268959744 | bytes 6291472 | tf_op jit(solution)/shard_map/while/body/eval_jaxpr/knta,knsb->ktsab/dot_general | solution.py:27
  143.6 9.3 %copy.35 = f32[16,4,4,64,64]{4,3,2,1,0:T(8,128)} copy(f32[16,4,4,64,64]{3,4,1,2,0:T(8,128)} %convolution_bitcast_fusion.2) | data formatting | bytes 8388608 | tf_op jit(solution)/shard_map/while/body/eval_jaxpr/knta,knsb->ktsab/transpose | solution.py:27
  152.9 7.9 %reshape.175 = f32[256,4096]{1,0:T(8,128)} reshape(f32[16,4,4,64,64]{4,3,2,1,0:T(8,128)} %copy.35) | data formatting | bytes 8388608 | tf_op jit(solution)/shard_map/while/body/eval_jaxpr/reshape | solution.py:30
  160.9 7.8 %scatter_fusion = f32[32,4096]{1,0:T(8,128)S(1)} fusion(f32[32,4096]{1,0:T(8,128)S(1)} %get-tuple-element.167, s32[256]{0:T(256)S(1)} %bitcast.69, f32[256,4096]{1,0:T(8,128)} %reshape.175), kind=kCustom, calls=%fused_computation.2.clone.1 | custom fusion | flops 1048576 | bytes 12583936 | tf_op jit(solution)/shard_map/while/body/eval_jaxpr/scatter-add | solution.py:31
  169.8 1.5 convolution_convert_fusion.2
  171.3 1.3 copy.33
  173.3 1.4 copy.34
  174.6 5.8 %convolution_bitcast_fusion.2 = f32[16,4,4,64,64]{3,4,1,2,0:T(8,128)} fusion(bf16[16,128,4,64,1]{1,3,4,2,0:T(8,128)(2,1)S(1)} %bitcast.63, bf16[16,128,4,64]{1,3,2,0:T(8,128)(2,1)} %bitcast.64, pred[16]{0:T(512)(128)(4,1)S(1)} %get-tuple-element.156), kind=kOutput, calls=%fused_computation.3.clone.1 | convolution fusion | flops 268959744 | bytes 6291472 | tf_op jit(solution)/shard_map/while/body/eval_jaxpr/knta,knsb->ktsab/dot_general | solution.py:27
  180.4 9.3 %copy.35 = f32[16,4,4,64,64]{4,3,2,1,0:T(8,128)} copy(f32[16,4,4,64,64]{3,4,1,2,0:T(8,128)} %convolution_bitcast_fusion.2) | data formatting | bytes 8388608 | tf_op jit(solution)/shard_map/while/body/eval_jaxpr/knta,knsb->ktsab/transpose | solution.py:27
  189.7 7.9 %reshape.175 = f32[256,4096]{1,0:T(8,128)} reshape(f32[16,4,4,64,64]{4,3,2,1,0:T(8,128)} %copy.35) | data formatting | bytes 8388608 | tf_op jit(solution)/shard_map/while/body/eval_jaxpr/reshape | solution.py:30
  197.7 7.8 %scatter_fusion = f32[32,4096]{1,0:T(8,128)S(1)} fusion(f32[32,4096]{1,0:T(8,128)S(1)} %get-tuple-element.167, s32[256]{0:T(256)S(1)} %bitcast.69, f32[256,4096]{1,0:T(8,128)} %reshape.175), kind=kCustom, calls=%fused_computation.2.clone.1 | custom fusion | flops 1048576 | bytes 12583936 | tf_op jit(solution)/shard_map/while/body/eval_jaxpr/scatter-add | solution.py:31
  206.6 1.5 convolution_convert_fusion.2
  210.0 1.4 copy.34
  211.4 5.8 %convolution_bitcast_fusion.2 = f32[16,4,4,64,64]{3,4,1,2,0:T(8,128)} fusion(bf16[16,128,4,64,1]{1,3,4,2,0:T(8,128)(2,1)S(1)} %bitcast.63, bf16[16,128,4,64]{1,3,2,0:T(8,128)(2,1)} %bitcast.64, pred[16]{0:T(512)(128)(4,1)S(1)} %get-tuple-element.156), kind=kOutput, calls=%fused_computation.3.clone.1 | convolution fusion | flops 268959744 | bytes 6291472 | tf_op jit(solution)/shard_map/while/body/eval_jaxpr/knta,knsb->ktsab/dot_general | solution.py:27
  217.2 9.3 %copy.35 = f32[16,4,4,64,64]{4,3,2,1,0:T(8,128)} copy(f32[16,4,4,64,64]{3,4,1,2,0:T(8,128)} %convolution_bitcast_fusion.2) | data formatting | bytes 8388608 | tf_op jit(solution)/shard_map/while/body/eval_jaxpr/knta,knsb->ktsab/transpose | solution.py:27
  226.5 7.9 %reshape.175 = f32[256,4096]{1,0:T(8,128)} reshape(f32[16,4,4,64,64]{4,3,2,1,0:T(8,128)} %copy.35) | data formatting | bytes 8388608 | tf_op jit(solution)/shard_map/while/body/eval_jaxpr/reshape | solution.py:30
  234.5 7.8 %scatter_fusion = f32[32,4096]{1,0:T(8,128)S(1)} fusion(f32[32,4096]{1,0:T(8,128)S(1)} %get-tuple-element.167, s32[256]{0:T(256)S(1)} %bitcast.69, f32[256,4096]{1,0:T(8,128)} %reshape.175), kind=kCustom, calls=%fused_computation.2.clone.1 | custom fusion | flops 1048576 | bytes 12583936 | tf_op jit(solution)/shard_map/while/body/eval_jaxpr/scatter-add | solution.py:31
  243.3 1.5 convolution_convert_fusion.2
  246.8 1.4 copy.34
  248.2 5.8 %convolution_bitcast_fusion.2 = f32[16,4,4,64,64]{3,4,1,2,0:T(8,128)} fusion(bf16[16,128,4,64,1]{1,3,4,2,0:T(8,128)(2,1)S(1)} %bitcast.63, bf16[16,128,4,64]{1,3,2,0:T(8,128)(2,1)} %bitcast.64, pred[16]{0:T(512)(128)(4,1)S(1)} %get-tuple-element.156), kind=kOutput, calls=%fused_computation.3.clone.1 | convolution fusion | flops 268959744 | bytes 6291472 | tf_op jit(solution)/shard_map/while/body/eval_jaxpr/knta,knsb->ktsab/dot_general | solution.py:27
  254.0 9.3 %copy.35 = f32[16,4,4,64,64]{4,3,2,1,0:T(8,128)} copy(f32[16,4,4,64,64]{3,4,1,2,0:T(8,128)} %convolution_bitcast_fusion.2) | data formatting | bytes 8388608 | tf_op jit(solution)/shard_map/while/body/eval_jaxpr/knta,knsb->ktsab/transpose | solution.py:27
  263.3 7.9 %reshape.175 = f32[256,4096]{1,0:T(8,128)} reshape(f32[16,4,4,64,64]{4,3,2,1,0:T(8,128)} %copy.35) | data formatting | bytes 8388608 | tf_op jit(solution)/shard_map/while/body/eval_jaxpr/reshape | solution.py:30
  271.3 7.8 %scatter_fusion = f32[32,4096]{1,0:T(8,128)S(1)} fusion(f32[32,4096]{1,0:T(8,128)S(1)} %get-tuple-element.167, s32[256]{0:T(256)S(1)} %bitcast.69, f32[256,4096]{1,0:T(8,128)} %reshape.175), kind=kCustom, calls=%fused_computation.2.clone.1 | custom fusion | flops 1048576 | bytes 12583936 | tf_op jit(solution)/shard_map/while/body/eval_jaxpr/scatter-add | solution.py:31
  279.1 26.4 %all-reduce.2 = bf16[32,4096]{1,0:T(8,128)(2,1)S(1)} all-reduce(f32[32,4096]{1,0:T(8,128)S(1)} %get-tuple-element.47), channel_id=2, replica_groups=mesh['row'=8,'col'=4] {'col'}, use_global_device_ids=true, to_apply=%region_3.4.clone | all-reduce | flops 131072 | bytes 786432
  (102 shorter events, 15.9 us)
Async XLA Ops:
  6.5 27.4 %all-gather.2.cloned.1.call-start = ((), (), s32[]{:S(2)}) async-start(), calls=%async_computation.1 | async-start | bytes 1179648 | tf_op jit(solution)/shard_map/all_gather | solution.py:52
  33.9 24.3 %all-to-all-start = ((bf16[4,2,2,128,256]{4,3,2,1,0:T(8,128)(2,1)}), bf16[4,2,2,128,256]{4,3,2,1,0:T(8,128)(2,1)S(1)}, u32[]{:S(2)}, u32[]{:S(2)}) async-start(bf16[4,2,2,128,256]{4,3,2,1,0:T(8,128)(2,1)} %bitcast.67), calls=%async_computation | async-start | bytes 2097152 | tf_op jit(solution)/shard_map/all_to_all | solution.py:54
  58.4 1.0 copy-start.1
  62.2 2.0 copy-start
  87.3 7.8 %copy-start.2 = (bf16[16,128,256]{2,1,0:T(8,128)(2,1)S(1)}, bf16[16,128,256]{2,1,0:T(8,128)(2,1)}, u32[]{:S(2)}) copy-start(bf16[16,128,256]{2,1,0:T(8,128)(2,1)} %copy-done.1) | copy-start | bytes 3145732 | tf_op jit(solution)/shard_map/while
  95.2 1.0 copy-start.1
  99.0 2.0 copy-start
  124.1 7.8 %copy-start.2 = (bf16[16,128,256]{2,1,0:T(8,128)(2,1)S(1)}, bf16[16,128,256]{2,1,0:T(8,128)(2,1)}, u32[]{:S(2)}) copy-start(bf16[16,128,256]{2,1,0:T(8,128)(2,1)} %copy-done.1) | copy-start | bytes 3145732 | tf_op jit(solution)/shard_map/while
  132.0 1.0 copy-start.1
  135.8 2.0 copy-start
  160.9 7.8 %copy-start.2 = (bf16[16,128,256]{2,1,0:T(8,128)(2,1)S(1)}, bf16[16,128,256]{2,1,0:T(8,128)(2,1)}, u32[]{:S(2)}) copy-start(bf16[16,128,256]{2,1,0:T(8,128)(2,1)} %copy-done.1) | copy-start | bytes 3145732 | tf_op jit(solution)/shard_map/while
  168.8 1.0 copy-start.1
  172.6 2.0 copy-start
  197.7 7.8 %copy-start.2 = (bf16[16,128,256]{2,1,0:T(8,128)(2,1)S(1)}, bf16[16,128,256]{2,1,0:T(8,128)(2,1)}, u32[]{:S(2)}) copy-start(bf16[16,128,256]{2,1,0:T(8,128)(2,1)} %copy-done.1) | copy-start | bytes 3145732 | tf_op jit(solution)/shard_map/while
  205.6 1.0 copy-start.1
  209.4 2.0 copy-start
  234.5 7.8 %copy-start.2 = (bf16[16,128,256]{2,1,0:T(8,128)(2,1)S(1)}, bf16[16,128,256]{2,1,0:T(8,128)(2,1)}, u32[]{:S(2)}) copy-start(bf16[16,128,256]{2,1,0:T(8,128)(2,1)} %copy-done.1) | copy-start | bytes 3145732 | tf_op jit(solution)/shard_map/while
  242.3 1.0 copy-start.1
  246.2 2.0 copy-start
  271.3 7.8 %copy-start.2 = (bf16[16,128,256]{2,1,0:T(8,128)(2,1)S(1)}, bf16[16,128,256]{2,1,0:T(8,128)(2,1)}, u32[]{:S(2)}) copy-start(bf16[16,128,256]{2,1,0:T(8,128)(2,1)} %copy-done.1) | copy-start | bytes 3145732 | tf_op jit(solution)/shard_map/while
Sparse Core Ops, SparseCore 0:
  8.9 24.9 all-gather.1
where the time goes:
time: 315 us; the launch traced here: 313 us
  local copies, waits for them, and re-layouts  133 us (42%)
  other arithmetic  49.7 us (16%)
  matrix products  44 us (14%)
  blocking collectives  40.7 us (13%)
  waiting for transfers between devices  27.4 us (9%)
  between operations  14.1 us (4%)
  starting transfers between devices  3.66 us (1%)
    transpose x6, local copies, waits for them, and re-layouts, accumulate(): jnp.einsum('knta,knsb->ktsab', left_split, right_split, preferred_element...  55.6 us
    reshape x6, local copies, waits for them, and re-layouts, accumulate(): contribs.reshape(group_size * agg_blocks * agg_blocks, agg_width * agg_wi...  47.4 us
    scatter-add x6, other arithmetic, accumulate(): running = running.at[sls.reshape(-1)].add(contribs)  46.8 us
    dot_general x6, matrix products, accumulate(): jnp.einsum('knta,knsb->ktsab', left_split, right_split, preferred_element...  34.7 us
    all_gather x1, waiting for transfers between devices, on_device(): column_rows = lax.all_gather(p_blocks, 'row', axis=0, tiled=True)  26.7 us
    unnamed x1, blocking collectives  26.4 us
    all_gather x1, blocking collectives, on_device(): row_panel = lax.all_gather(p_blocks, 'col', axis=0, tiled=True)  14.3 us
    gather x12, local copies, waits for them, and re-layouts, accumulate(): left_rows = jnp.take(row_panel, rws, axis=0)  12 us
  transfers between devices with their start and end apart: 2, of which 1 were waited for; matrix products, arithmetic and copies ran while one was open for 2% of the time, Pallas kernels for 0%

commit v1 on v0

v1 whole, which is shorter than its diff:
```python
from functools import partial

import jax
import jax.numpy as jnp
from jax import lax
from jax.experimental import pallas as pl
from jax.experimental.pallas import tpu as pltpu
from jax.sharding import PartitionSpec as P

KS_DEV = 8
N_ACC = 4
VMEM = pl.BlockSpec(memory_space=pltpu.VMEM)
SMEM = pl.BlockSpec(memory_space=pltpu.SMEM)
F32 = jnp.float32
BF16 = jnp.bfloat16


def iota(shape, axis):
    return lax.broadcasted_iota(jnp.int32, shape, axis)


def unroll_of(count, most):
    return max(u for u in range(1, most + 1) if count % u == 0)


def left_kernel(n_parts, agg_blocks, rows_ref, *refs):
    parts, (blocks_ref, left_ref, turned) = refs[:n_parts], refs[n_parts:]
    per_part, node, width = parts[0].shape
    agg = width // agg_blocks
    half = agg // 2
    tall = agg_blocks * half
    out_row, in_col = iota((width, width), 0), iota((width, width), 1)
    within = out_row % tall
    wanted = (within // half) * agg + 2 * (within % half) + out_row // tall
    order = jnp.where(in_col == wanted, 1.0, 0.0).astype(BF16)
    me = lax.axis_index("col")
    for step, part in enumerate(parts):
        source = lax.rem(me - step + n_parts, n_parts)
        for e in range(per_part):
            turned[source * per_part + e] = lax.dot_general(
                order, part[e], (((1,), (1,)), ((), ())), preferred_element_type=F32
            ).astype(BF16)

    count = blocks_ref.shape[0]

    def one(k, _):
        both = jnp.dot(turned[rows_ref[k]], blocks_ref[k], preferred_element_type=F32).astype(BF16)
        left_ref[k, :, :node] = both[:tall]
        left_ref[k, :, node:] = both[tall:]
        return 0

    lax.fori_loop(0, count, one, 0, unroll=unroll_of(count, 8))


def sum_kernel(n_cols, fan, agg_blocks, cols_ref, slots_ref, *refs):
    n_parts = n_cols * fan
    parts, left_ref = refs[:n_parts], refs[n_parts]
    own_ref, sent_refs = refs[n_parts + 1], refs[n_parts + 2 : n_parts + 1 + n_cols]
    wide, accs = refs[n_parts + 1 + n_cols], refs[n_parts + 2 + n_cols :]
    per_part, node, width = parts[0].shape
    agg = width // agg_blocks
    half = agg // 2
    for acc in accs:
        acc[...] = jnp.zeros_like(acc)
    row = lax.axis_index("row")
    mine, line = lax.rem(row, fan), lax.div(row, fan)
    src, dst = iota((width, 2 * width), 0), iota((width, 2 * width), 1)
    spread = [
        jnp.where(dst == (src // agg) * 2 * agg + h * agg + src % agg, 1.0, 0.0).astype(BF16)
        for h in range(2)
    ]
    for g in range(fan):
        owner = lax.rem(mine - g + fan, fan)
        for step in range(n_cols):
            source = lax.rem(line - step + n_cols, n_cols)
            for e in range(per_part):
                j = (owner * n_cols + source) * per_part + e
                piece = parts[g * n_cols + step][e]
                for h in range(2):
                    wide[j, h * node : (h + 1) * node] = jnp.dot(
                        piece, spread[h], preferred_element_type=F32
                    ).astype(BF16)

    count = left_ref.shape[0]
    pairs = agg_blocks * agg_blocks

    def one(k, _):
        term = jnp.dot(left_ref[k], wide[cols_ref[k]], preferred_element_type=F32)
        for t in range(agg_blocks):
            for s in range(agg_blocks):
                slot = slots_ref[k * pairs + t * agg_blocks + s]
                acc = accs[(t * agg_blocks + s) % len(accs)]
                acc[slot] += term[t * half : (t + 1) * half, s * 2 * agg : (s + 1) * 2 * agg]
        return 0

    lax.fori_loop(0, count, one, 0, unroll=unroll_of(count, 16))

    me = lax.axis_index("col")
    for step in range(n_cols):
        first = lax.rem(me + step, n_cols) * KS_DEV
        total = accs[0][pl.ds(first, KS_DEV)]
        for acc in accs[1:]:
            total += acc[pl.ds(first, KS_DEV)]
        if step == 0:
            own_ref[...] = total
        else:
            sent_refs[step - 1][...] = total.astype(BF16)


def final_kernel(own_ref, *refs):
    got, out_ref = refs[:-1], refs[-1]
    lanes = own_ref.shape[2]
    for a in range(own_ref.shape[1]):
        total = own_ref[:, a, :]
        for part in got:
            total += part[:, a, :].astype(F32)
        out_ref[0, :, a * lanes : (a + 1) * lanes] = total.astype(BF16)


def on_device(a_blocks, a_rows, a_cols, p_blocks, coarse_slot):
    rows_total = lax.axis_size("row")
    cols_total = lax.axis_size("col")
    fan = rows_total // cols_total
    per_part, node, width = p_blocks.shape
    count = a_blocks.shape[2]
    agg_blocks = coarse_slot.shape[3]
    agg = width // agg_blocks
    both = ("row", "col")

    def shift(x, axis, d, n):
        return lax.ppermute(x, axis, [(i, (i + d) % n) for i in range(n)])

    row_parts = [p_blocks] + [shift(p_blocks, "col", d, cols_total) for d in range(1, cols_total)]
    direct = []
    for d in range(cols_total):
        pairs = []
        for c in range(cols_total):
            for f in range(fan):
                for x in range(cols_total):
                    target = ((x + d) % cols_total) * fan + f
                    pairs.append(((c * fan + f) * cols_total + x, target * cols_total + c))
        direct.append(lax.ppermute(p_blocks, both, pairs))
    col_parts = list(direct)
    for g in range(1, fan):
        swap = [(r, (r // fan) * fan + (r % fan + g) % fan) for r in range(rows_total)]
        col_parts += [lax.ppermute(part, "row", swap) for part in direct]

    left = pl.pallas_call(
        partial(left_kernel, cols_total, agg_blocks),
        out_shape=jax.ShapeDtypeStruct((count, width // 2, 2 * node), BF16),
        in_specs=[SMEM] + [VMEM] * (cols_total + 1),
        out_specs=VMEM,
        scratch_shapes=[pltpu.VMEM((per_part * cols_total, width, node), BF16)],
        name="left",
    )(a_rows.reshape(-1), *row_parts, a_blocks.reshape(a_blocks.shape[2:]))

    slot_count = KS_DEV * cols_total
    chunk = (KS_DEV, agg // 2, 2 * agg)
    sums = pl.pallas_call(
        partial(sum_kernel, cols_total, fan, agg_blocks),
        out_shape=[jax.ShapeDtypeStruct(chunk, F32)]
        + [jax.ShapeDtypeStruct(chunk, BF16)] * (cols_total - 1),
        in_specs=[SMEM] * 2 + [VMEM] * (cols_total * fan + 1),
        out_specs=[VMEM] * cols_total,
        scratch_shapes=[pltpu.VMEM((per_part * cols_total * fan, 2 * node, 2 * width), BF16)]
        + [pltpu.VMEM((slot_count,) + chunk[1:], F32)] * N_ACC,
        name="sums",
    )(a_cols.reshape(-1), coarse_slot.reshape(-1), *col_parts, left)
    got = [shift(part, "col", d, cols_total) for d, part in enumerate(sums[1:], 1)]
    return pl.pallas_call(
        final_kernel,
        out_shape=jax.ShapeDtypeStruct((1, KS_DEV, agg * agg), BF16),
        in_specs=[VMEM] * cols_total,
        out_specs=VMEM,
        name="final",
    )(sums[0], *got)


def solution(mesh):
    placed = (
        P("row", "col", None, None, None),
        P("row", "col", None),
        P("row", "col", None),
        P(("row", "col"), None, None),
        P("row", "col", None, None, None),
    )
    return jax.shard_map(
        on_device, mesh=mesh, in_specs=placed, out_specs=P("row", "col", None), check_vma=False
    )
```

time: 315 us -> 56.3 us (0.18)
  local copies, waits for them, and re-layouts: 133 us -> 3.62 us
  other arithmetic: 49.7 us -> 0 us
  matrix products: 44 us -> 0 us
  blocking collectives: 40.7 us -> 0 us
  starting transfers between devices: 3.66 us -> 27.4 us
  waiting for transfers between devices: 27.4 us -> 4.24 us
  Pallas kernels: 0 us -> 20.6 us
  between operations: 14.1 us -> 0.14 us
    transpose x6 -> x0, local copies, waits for them, and re-layouts: 55.6 us -> none  [accumulate(): jnp.einsum('knta,knsb->ktsab', left_split, right_split, preferred_element...]
    reshape x12 -> x1, local copies, waits for them, and re-layouts: 48 us -> 0.8 us  [on_device(): coarse_slot.reshape(-1)]
    scatter-add x6 -> x0, other arithmetic: 46.8 us -> none  [accumulate(): running = running.at[sls.reshape(-1)].add(contribs)]
    dot_general x12 -> x0, matrix products: 44 us -> none  [the longest x6 34.7 us: accumulate(): jnp.einsum('knta,knsb->ktsab', left_split, right_split, preferred_element...]
    ppermute x0 -> x14, starting transfers between devices: none -> 27.4 us  [the longest x6 14.2 us: shift(): return lax.ppermute(x, axis, [(i, (i + d) % n) for i in range(n)])]
    all_gather x1 -> x0, waiting for transfers between devices: 26.7 us -> none  [on_device(): column_rows = lax.all_gather(p_blocks, 'row', axis=0, tiled=True)]
    unnamed x1 -> x0, blocking collectives: 26.4 us -> none
    pallas_call x0 -> x3, Pallas kernels: none -> 20.6 us  [the longest x1 9.91 us: on_device(): pl.pallas_call(partial(sum_kernel, cols_total, fan, agg_blocks), out_shap...]
  transfers between devices with their start and end apart: 2 -> 14, of which waited for: 1 -> 3; matrix products, arithmetic and copies ran while one was open for 2% -> 3% of each run, Pallas kernels for 0% -> 16%
where the time goes in v1:
time: 56.3 us; the launch traced here: 56 us
  starting transfers between devices  27.4 us (49%)
  Pallas kernels  20.6 us (37%)
  waiting for transfers between devices  4.24 us (8%)
  local copies, waits for them, and re-layouts  3.62 us (6%)
    ppermute x6, starting transfers between devices, shift(): return lax.ppermute(x, axis, [(i, (i + d) % n) for i in range(n)])  14.2 us
    ppermute x4, starting transfers between devices, on_device(): direct.append(lax.ppermute(p_blocks, both, pairs))  12.2 us
    pallas_call x1, Pallas kernels, on_device(): pl.pallas_call(partial(sum_kernel, cols_total, fan, agg_blocks), out_shap...  9.91 us
    pallas_call x1, Pallas kernels, on_device(): pl.pallas_call(partial(left_kernel, cols_total, agg_blocks), out_shape=ja...  8.69 us
    ppermute x6, waiting for transfers between devices, shift(): return lax.ppermute(x, axis, [(i, (i + d) % n) for i in range(n)])  4.22 us
    unnamed x29, local copies, waits for them, and re-layouts  2.82 us
    pallas_call x1, Pallas kernels, on_device(): pl.pallas_call(final_kernel, out_shape=jax.ShapeDtypeStruct((1, KS_DEV, a...  2.01 us
  transfers between devices with their start and end apart: 14, of which 3 were waited for; matrix products, arithmetic and copies ran while one was open for 3% of the time, Pallas kernels for 16%

profile of v1, /device:TPU:0, one launch (start us, length us, event | category | flops | bytes accessed | tf_op | source)
XLA Modules:
  0.0 56.0 jit_solution(925660807215323258)
XLA Ops:
  0.0 1.6 %collective-permute-start = (bf16[2,128,256]{2,1,0:T(8,128)(2,1)}, bf16[2,128,256]{2,1,0:T(8,128)(2,1)S(1)}, u32[]{:S(2)}, u32[]{:S(2)}) collective-permute-start(bf16[2,128,256]{2,1,0:T(8,128)(2,1)} %refs_0_.1), channel_id=1, source_target_pairs={{0,0},{1,8},{2,16},{3,24},{4,4},{5,12},{6,20},{7,28},{8,1},{9,9},{... | collective-permute-start | bytes 393224 | tf_op jit(solution)/shard_map/ppermute | solution.py:142
  1.6 4.8 %collective-permute-start.1 = (bf16[2,128,256]{2,1,0:T(8,128)(2,1)}, bf16[2,128,256]{2,1,0:T(8,128)(2,1)S(1)}, u32[]{:S(2)}, u32[]{:S(2)}) collective-permute-start(bf16[2,128,256]{2,1,0:T(8,128)(2,1)} %refs_0_.1), channel_id=1, source_target_pairs={{0,8},{1,16},{2,24},{3,0},{4,12},{5,20},{6,28},{7,4},{8,9},{9,17},... | collective-permute-start | bytes 393224 | tf_op jit(solution)/shard_map/ppermute | solution.py:142
  6.4 3.5 %collective-permute-start.2 = (bf16[2,128,256]{2,1,0:T(8,128)(2,1)}, bf16[2,128,256]{2,1,0:T(8,128)(2,1)S(1)}, u32[]{:S(2)}, u32[]{:S(2)}) collective-permute-start(bf16[2,128,256]{2,1,0:T(8,128)(2,1)} %refs_0_.1), channel_id=1, source_target_pairs={{0,16},{1,24},{2,0},{3,8},{4,20},{5,28},{6,4},{7,12},{8,17},{9,25}... | collective-permute-start | bytes 393224 | tf_op jit(solution)/shard_map/ppermute | solution.py:142
  9.9 2.3 %collective-permute-start.3 = (bf16[2,128,256]{2,1,0:T(8,128)(2,1)}, bf16[2,128,256]{2,1,0:T(8,128)(2,1)S(1)}, u32[]{:S(2)}, u32[]{:S(2)}) collective-permute-start(bf16[2,128,256]{2,1,0:T(8,128)(2,1)} %refs_0_.1), channel_id=1, source_target_pairs={{0,24},{1,0},{2,8},{3,16},{4,28},{5,4},{6,12},{7,20},{8,25},{9,1},... | collective-permute-start | bytes 393224 | tf_op jit(solution)/shard_map/ppermute | solution.py:142
  12.2 0.7 %collective-permute-start.10 = (bf16[2,128,256]{2,1,0:T(8,128)(2,1)}, bf16[2,128,256]{2,1,0:T(8,128)(2,1)S(1)}, u32[]{:S(2)}, u32[]{:S(2)}) collective-permute-start(bf16[2,128,256]{2,1,0:T(8,128)(2,1)} %refs_0_.1), channel_id=1, source_target_pairs={{0,3},{1,0},{2,1},{3,2},{4,7},{5,4},{6,5},{7,6},{8,11},{9,8},{10,9... | collective-permute-start | bytes 393224 | tf_op jit(solution)/shard_map/ppermute | solution.py:131
  12.9 0.0 collective-permute-done.refs_0_
  12.9 3.1 %collective-permute-start.8 = (bf16[2,128,256]{2,1,0:T(8,128)(2,1)}, bf16[2,128,256]{2,1,0:T(8,128)(2,1)S(1)}, u32[]{:S(2)}, u32[]{:S(2)}) collective-permute-start(bf16[2,128,256]{2,1,0:T(8,128)(2,1)} %refs_0_.1), channel_id=1, source_target_pairs={{0,1},{1,2},{2,3},{3,0},{4,5},{5,6},{6,7},{7,4},{8,9},{9,10},{10,1... | collective-permute-start | bytes 393224 | tf_op jit(solution)/shard_map/ppermute | solution.py:131
  16.0 0.0 collective-permute-done.1.refs_1_
  16.0 5.0 %collective-permute-start.9 = (bf16[2,128,256]{2,1,0:T(8,128)(2,1)}, bf16[2,128,256]{2,1,0:T(8,128)(2,1)S(1)}, u32[]{:S(2)}, u32[]{:S(2)}) collective-permute-start(bf16[2,128,256]{2,1,0:T(8,128)(2,1)} %refs_0_.1), channel_id=1, source_target_pairs={{0,2},{1,3},{2,0},{3,1},{4,6},{5,7},{6,4},{7,5},{8,10},{9,11},{10,... | collective-permute-start | bytes 393224 | tf_op jit(solution)/shard_map/ppermute | solution.py:131
  21.0 0.0 collective-permute-done.2.refs_2_
  21.0 0.0 collective-permute-start.4
  21.0 0.0 collective-permute-done.3.refs_3_
  21.0 0.0 copy-start.3
  21.0 0.5 collective-permute-start.5
  21.5 1.6 %collective-permute-done.10.refs_3_ = bf16[2,128,256]{2,1,0:T(8,128)(2,1)S(1)} collective-permute-done((bf16[2,128,256]{2,1,0:T(8,128)(2,1)}, bf16[2,128,256]{2,1,0:T(8,128)(2,1)S(1)}, u32[]{:S(2)}, u32[]{:S(2)}) %collective-permute-start.10) | collective-permute-done | bytes 131104 | tf_op jit(solution)/shard_map/ppermute | solution.py:131
  23.1 0.0 collective-permute-start.6
  23.1 0.0 collective-permute-done.8.refs_1_
  23.1 0.0 copy-start.7
  23.1 0.5 collective-permute-start.7
  23.6 0.8 %copy.6 = s32[1,1,96,4,4]{4,3,2,1,0:T(4,128)S(1)} copy(s32[1,1,96,4,4]{2,4,3,1,0:T(4,128)} %param.9) | data formatting | bytes 12288 | tf_op args[4]
  24.4 0.8 %reshape.13.slots_ref = s32[1536]{0:T(1024)} reshape(s32[1,1,96,4,4]{4,3,2,1,0:T(4,128)S(1)} %copy.6) | data formatting | bytes 12288 | tf_op jit(solution)/shard_map/reshape | solution.py:168
  25.2 0.0 collective-permute-done.9.refs_2_
  25.2 0.0 copy-done.5
  25.2 0.0 copy-done.7
  25.3 0.6 %copy-done.9 = bf16[2,128,256]{2,1,0:T(8,128)(2,1)} copy-done((bf16[2,128,256]{2,1,0:T(8,128)(2,1)}, bf16[2,128,256]{2,1,0:T(8,128)(2,1)S(1)}, u32[]{:S(2)}) %copy-start.9) | copy-done | bytes 131096
  25.9 8.7 %left.1.refs_8_ = bf16[96,128,256]{2,1,0:T(8,128)(2,1)} custom-call(s32[96]{0:T(128)} %bitcast.4, bf16[2,128,256]{2,1,0:T(8,128)(2,1)} %refs_0_.1, bf16[2,128,256]{2,1,0:T(8,128)(2,1)} %copy-done.7, bf16[2,128,256]{2,1,0:T(8,128)(2,1)} %copy-done.9, bf16[2,128,256]{2,1,0:T(8,128)(2,1)} %copy-done.5, bf16[96,128,128]{2,1,0:T(8,128)(2,1)} %bitcast.3), custom_call_target="tpu_custom_call" | custom-call | tf_op jit(solution)/shard_map/left/pallas_call | solution.py:148
  34.6 0.0 collective-permute-done.4.refs_4_
  34.6 0.0 collective-permute-done.5.refs_5_
  34.6 0.0 copy-start.6
  34.6 0.0 collective-permute-done.6.refs_6_
  34.6 0.0 copy-start.8
  34.6 0.0 collective-permute-done.7.refs_7_
  34.6 0.0 copy-start.10
  34.7 0.0 copy-done
  34.7 0.6 copy-done.4
  35.2 0.1 copy-done.6
  35.3 0.0 copy-done.8
  35.3 0.0 copy-done.10
  35.4 9.9 %sums.1 = (f32[8,32,128]{2,1,0:T(8,128)}, bf16[8,32,128]{2,1,0:T(8,128)(2,1)}, bf16[8,32,128]{2,1,0:T(8,128)(2,1)}, bf16[8,32,128]{2,1,0:T(8,128)(2,1)}) custom-call(s32[96]{0:T(128)} %bitcast.5, s32[1536]{0:T(1024)} %reshape.13.slots_ref, bf16[2,128,256]{2,1,0:T(8,128)(2,1)} %copy-done, bf16[2,128,256]{2,1,0:T(8,128)(2,1)} %copy-done.1, ...), custom_call_target="tpu_custom_call" | custom-call | tf_op jit(solution)/shard_map/sums/pallas_call | solution.py:159
  45.3 0.6 %collective-permute-start.11 = (bf16[8,32,128]{2,1,0:T(8,128)(2,1)}, bf16[8,32,128]{2,1,0:T(8,128)(2,1)S(1)}, u32[]{:S(2)}, u32[]{:S(2)}) collective-permute-start(bf16[8,32,128]{2,1,0:T(8,128)(2,1)} %get-tuple-element.10), channel_id=1, source_target_pairs={{0,1},{1,2},{2,3},{3,0},{4,5},{5,6},{6,7},{7,4},{8,9},{9,10},{10,1... | collective-permute-start | bytes 196616 | tf_op jit(solution)/shard_map/ppermute | solution.py:131
  45.9 2.0 %collective-permute-start.12 = (bf16[8,32,128]{2,1,0:T(8,128)(2,1)}, bf16[8,32,128]{2,1,0:T(8,128)(2,1)S(1)}, u32[]{:S(2)}, u32[]{:S(2)}) collective-permute-start(bf16[8,32,128]{2,1,0:T(8,128)(2,1)} %get-tuple-element.11), channel_id=1, source_target_pairs={{0,2},{1,3},{2,0},{3,1},{4,6},{5,7},{6,4},{7,5},{8,10},{9,11},{10,... | collective-permute-start | bytes 196616 | tf_op jit(solution)/shard_map/ppermute | solution.py:131
  47.9 2.9 %collective-permute-start.13 = (bf16[8,32,128]{2,1,0:T(8,128)(2,1)}, bf16[8,32,128]{2,1,0:T(8,128)(2,1)S(1)}, u32[]{:S(2)}, u32[]{:S(2)}) collective-permute-start(bf16[8,32,128]{2,1,0:T(8,128)(2,1)} %get-tuple-element.12), channel_id=1, source_target_pairs={{0,3},{1,0},{2,1},{3,2},{4,7},{5,4},{6,5},{7,6},{8,11},{9,8},{10,9... | collective-permute-start | bytes 196616 | tf_op jit(solution)/shard_map/ppermute | solution.py:131
  50.8 0.0 collective-permute-done.11.refs_0_
  50.8 1.1 %collective-permute-done.12.refs_1_ = bf16[8,32,128]{2,1,0:T(8,128)(2,1)S(1)} collective-permute-done((bf16[8,32,128]{2,1,0:T(8,128)(2,1)}, bf16[8,32,128]{2,1,0:T(8,128)(2,1)S(1)}, u32[]{:S(2)}, u32[]{:S(2)}) %collective-permute-start.12) | collective-permute-done | bytes 65568 | tf_op jit(solution)/shard_map/ppermute | solution.py:131
  51.9 1.5 %collective-permute-done.13.refs_2_ = bf16[8,32,128]{2,1,0:T(8,128)(2,1)S(1)} collective-permute-done((bf16[8,32,128]{2,1,0:T(8,128)(2,1)}, bf16[8,32,128]{2,1,0:T(8,128)(2,1)S(1)}, u32[]{:S(2)}, u32[]{:S(2)}) %collective-permute-start.13) | collective-permute-done | bytes 65568 | tf_op jit(solution)/shard_map/ppermute | solution.py:131
  53.4 0.0 copy-done.11
  53.4 0.6 %copy-done.13 = bf16[8,32,128]{2,1,0:T(8,128)(2,1)} copy-done((bf16[8,32,128]{2,1,0:T(8,128)(2,1)}, bf16[8,32,128]{2,1,0:T(8,128)(2,1)S(1)}, u32[]{:S(2)}) %copy-start.13) | copy-done | bytes 65560
  54.0 2.0 %final.1 = bf16[1,8,4096]{2,1,0:T(8,128)(2,1)} custom-call(f32[8,32,128]{2,1,0:T(8,128)} %get-tuple-element.9.own_ref, bf16[8,32,128]{2,1,0:T(8,128)(2,1)} %copy-done.11, bf16[8,32,128]{2,1,0:T(8,128)(2,1)} %copy-done.12, bf16[8,32,128]{2,1,0:T(8,128)(2,1)} %copy-done.13), custom_call_target="tpu_custom_call" | custom-call | tf_op jit(solution)/shard_map/final/pallas_call | solution.py:170
  (13 shorter events, 0.0 us)
Async XLA Ops:
  0.0 12.9 %collective-permute-start = (bf16[2,128,256]{2,1,0:T(8,128)(2,1)}, bf16[2,128,256]{2,1,0:T(8,128)(2,1)S(1)}, u32[]{:S(2)}, u32[]{:S(2)}) collective-permute-start(bf16[2,128,256]{2,1,0:T(8,128)(2,1)} %refs_0_.1), channel_id=1, source_target_pairs={{0,0},{1,8},{2,16},{3,24},{4,4},{5,12},{6,20},{7,28},{8,1},{9,9},{... | collective-permute-start | bytes 393224 | tf_op jit(solution)/shard_map/ppermute | solution.py:142
  1.6 14.4 %collective-permute-start.1 = (bf16[2,128,256]{2,1,0:T(8,128)(2,1)}, bf16[2,128,256]{2,1,0:T(8,128)(2,1)S(1)}, u32[]{:S(2)}, u32[]{:S(2)}) collective-permute-start(bf16[2,128,256]{2,1,0:T(8,128)(2,1)} %refs_0_.1), channel_id=1, source_target_pairs={{0,8},{1,16},{2,24},{3,0},{4,12},{5,20},{6,28},{7,4},{8,9},{9,17},... | collective-permute-start | bytes 393224 | tf_op jit(solution)/shard_map/ppermute | solution.py:142
  6.4 14.6 %collective-permute-start.2 = (bf16[2,128,256]{2,1,0:T(8,128)(2,1)}, bf16[2,128,256]{2,1,0:T(8,128)(2,1)S(1)}, u32[]{:S(2)}, u32[]{:S(2)}) collective-permute-start(bf16[2,128,256]{2,1,0:T(8,128)(2,1)} %refs_0_.1), channel_id=1, source_target_pairs={{0,16},{1,24},{2,0},{3,8},{4,20},{5,28},{6,4},{7,12},{8,17},{9,25}... | collective-permute-start | bytes 393224 | tf_op jit(solution)/shard_map/ppermute | solution.py:142
  9.9 11.1 %collective-permute-start.3 = (bf16[2,128,256]{2,1,0:T(8,128)(2,1)}, bf16[2,128,256]{2,1,0:T(8,128)(2,1)S(1)}, u32[]{:S(2)}, u32[]{:S(2)}) collective-permute-start(bf16[2,128,256]{2,1,0:T(8,128)(2,1)} %refs_0_.1), channel_id=1, source_target_pairs={{0,24},{1,0},{2,8},{3,16},{4,28},{5,4},{6,12},{7,20},{8,25},{9,1},... | collective-permute-start | bytes 393224 | tf_op jit(solution)/shard_map/ppermute | solution.py:142
  12.2 10.9 %collective-permute-start.10 = (bf16[2,128,256]{2,1,0:T(8,128)(2,1)}, bf16[2,128,256]{2,1,0:T(8,128)(2,1)S(1)}, u32[]{:S(2)}, u32[]{:S(2)}) collective-permute-start(bf16[2,128,256]{2,1,0:T(8,128)(2,1)} %refs_0_.1), channel_id=1, source_target_pairs={{0,3},{1,0},{2,1},{3,2},{4,7},{5,4},{6,5},{7,6},{8,11},{9,8},{10,9... | collective-permute-start | bytes 393224 | tf_op jit(solution)/shard_map/ppermute | solution.py:131
  12.9 21.8 %copy-start = (bf16[2,128,256]{2,1,0:T(8,128)(2,1)}, bf16[2,128,256]{2,1,0:T(8,128)(2,1)S(1)}, u32[]{:S(2)}) copy-start(bf16[2,128,256]{2,1,0:T(8,128)(2,1)S(1)} %collective-permute-done.refs_0_) | copy-start | bytes 393220
  12.9 10.2 %collective-permute-start.8 = (bf16[2,128,256]{2,1,0:T(8,128)(2,1)}, bf16[2,128,256]{2,1,0:T(8,128)(2,1)S(1)}, u32[]{:S(2)}, u32[]{:S(2)}) collective-permute-start(bf16[2,128,256]{2,1,0:T(8,128)(2,1)} %refs_0_.1), channel_id=1, source_target_pairs={{0,1},{1,2},{2,3},{3,0},{4,5},{5,6},{6,7},{7,4},{8,9},{9,10},{10,1... | collective-permute-start | bytes 393224 | tf_op jit(solution)/shard_map/ppermute | solution.py:131
  16.0 18.7 %copy-start.1 = (bf16[2,128,256]{2,1,0:T(8,128)(2,1)}, bf16[2,128,256]{2,1,0:T(8,128)(2,1)S(1)}, u32[]{:S(2)}) copy-start(bf16[2,128,256]{2,1,0:T(8,128)(2,1)S(1)} %collective-permute-done.1.refs_1_) | copy-start | bytes 393220
  16.0 9.2 %collective-permute-start.9 = (bf16[2,128,256]{2,1,0:T(8,128)(2,1)}, bf16[2,128,256]{2,1,0:T(8,128)(2,1)S(1)}, u32[]{:S(2)}, u32[]{:S(2)}) collective-permute-start(bf16[2,128,256]{2,1,0:T(8,128)(2,1)} %refs_0_.1), channel_id=1, source_target_pairs={{0,2},{1,3},{2,0},{3,1},{4,6},{5,7},{6,4},{7,5},{8,10},{9,11},{10,... | collective-permute-start | bytes 393224 | tf_op jit(solution)/shard_map/ppermute | solution.py:131
  21.0 13.7 %copy-start.2 = (bf16[2,128,256]{2,1,0:T(8,128)(2,1)}, bf16[2,128,256]{2,1,0:T(8,128)(2,1)S(1)}, u32[]{:S(2)}) copy-start(bf16[2,128,256]{2,1,0:T(8,128)(2,1)S(1)} %collective-permute-done.2.refs_2_) | copy-start | bytes 393220
  21.0 13.6 %collective-permute-start.4 = (bf16[2,128,256]{2,1,0:T(8,128)(2,1)S(1)}, bf16[2,128,256]{2,1,0:T(8,128)(2,1)S(1)}, u32[]{:S(2)}, u32[]{:S(2)}) collective-permute-start(bf16[2,128,256]{2,1,0:T(8,128)(2,1)S(1)} %collective-permute-done.refs_0_), channel_id=1, source_target_pairs={{0,4},{4,0},{8,12},{12,8},{16,20},{20,16},{24,28},{28,24},{1,5},{5... | collective-permute-start | bytes 393224 | tf_op jit(solution)/shard_map/ppermute | solution.py:146
  21.0 13.7 %copy-start.3 = (bf16[2,128,256]{2,1,0:T(8,128)(2,1)}, bf16[2,128,256]{2,1,0:T(8,128)(2,1)S(1)}, u32[]{:S(2)}) copy-start(bf16[2,128,256]{2,1,0:T(8,128)(2,1)S(1)} %collective-permute-done.3.refs_3_) | copy-start | bytes 393220
  21.0 13.6 %collective-permute-start.5 = (bf16[2,128,256]{2,1,0:T(8,128)(2,1)S(1)}, bf16[2,128,256]{2,1,0:T(8,128)(2,1)S(1)}, u32[]{:S(2)}, u32[]{:S(2)}) collective-permute-start(bf16[2,128,256]{2,1,0:T(8,128)(2,1)S(1)} %collective-permute-done.1.refs_1_), channel_id=1, source_target_pairs={{0,4},{4,0},{8,12},{12,8},{16,20},{20,16},{24,28},{28,24},{1,5},{5... | collective-permute-start | bytes 393224 | tf_op jit(solution)/shard_map/ppermute | solution.py:146
  23.1 2.2 %copy-start.5 = (bf16[2,128,256]{2,1,0:T(8,128)(2,1)}, bf16[2,128,256]{2,1,0:T(8,128)(2,1)S(1)}, u32[]{:S(2)}) copy-start(bf16[2,128,256]{2,1,0:T(8,128)(2,1)S(1)} %collective-permute-done.10.refs_3_) | copy-start | bytes 393220
  23.1 11.5 %collective-permute-start.6 = (bf16[2,128,256]{2,1,0:T(8,128)(2,1)S(1)}, bf16[2,128,256]{2,1,0:T(8,128)(2,1)S(1)}, u32[]{:S(2)}, u32[]{:S(2)}) collective-permute-start(bf16[2,128,256]{2,1,0:T(8,128)(2,1)S(1)} %collective-permute-done.2.refs_2_), channel_id=1, source_target_pairs={{0,4},{4,0},{8,12},{12,8},{16,20},{20,16},{24,28},{28,24},{1,5},{5... | collective-permute-start | bytes 393224 | tf_op jit(solution)/shard_map/ppermute | solution.py:146
  23.1 2.2 %copy-start.7 = (bf16[2,128,256]{2,1,0:T(8,128)(2,1)}, bf16[2,128,256]{2,1,0:T(8,128)(2,1)S(1)}, u32[]{:S(2)}) copy-start(bf16[2,128,256]{2,1,0:T(8,128)(2,1)S(1)} %collective-permute-done.8.refs_1_) | copy-start | bytes 393220
  23.1 11.5 %collective-permute-start.7 = (bf16[2,128,256]{2,1,0:T(8,128)(2,1)S(1)}, bf16[2,128,256]{2,1,0:T(8,128)(2,1)S(1)}, u32[]{:S(2)}, u32[]{:S(2)}) collective-permute-start(bf16[2,128,256]{2,1,0:T(8,128)(2,1)S(1)} %collective-permute-done.3.refs_3_), channel_id=1, source_target_pairs={{0,4},{4,0},{8,12},{12,8},{16,20},{20,16},{24,28},{28,24},{1,5},{5... | collective-permute-start | bytes 393224 | tf_op jit(solution)/shard_map/ppermute | solution.py:146
  25.2 0.7 %copy-start.9 = (bf16[2,128,256]{2,1,0:T(8,128)(2,1)}, bf16[2,128,256]{2,1,0:T(8,128)(2,1)S(1)}, u32[]{:S(2)}) copy-start(bf16[2,128,256]{2,1,0:T(8,128)(2,1)S(1)} %collective-permute-done.9.refs_2_) | copy-start | bytes 393220
  34.6 0.7 %copy-start.4 = (bf16[2,128,256]{2,1,0:T(8,128)(2,1)}, bf16[2,128,256]{2,1,0:T(8,128)(2,1)S(1)}, u32[]{:S(2)}) copy-start(bf16[2,128,256]{2,1,0:T(8,128)(2,1)S(1)} %collective-permute-done.4.refs_4_) | copy-start | bytes 393220
  34.6 0.7 %copy-start.6 = (bf16[2,128,256]{2,1,0:T(8,128)(2,1)}, bf16[2,128,256]{2,1,0:T(8,128)(2,1)S(1)}, u32[]{:S(2)}) copy-start(bf16[2,128,256]{2,1,0:T(8,128)(2,1)S(1)} %collective-permute-done.5.refs_5_) | copy-start | bytes 393220
  34.6 0.7 %copy-start.8 = (bf16[2,128,256]{2,1,0:T(8,128)(2,1)}, bf16[2,128,256]{2,1,0:T(8,128)(2,1)S(1)}, u32[]{:S(2)}) copy-start(bf16[2,128,256]{2,1,0:T(8,128)(2,1)S(1)} %collective-permute-done.6.refs_6_) | copy-start | bytes 393220
  34.6 0.7 %copy-start.10 = (bf16[2,128,256]{2,1,0:T(8,128)(2,1)}, bf16[2,128,256]{2,1,0:T(8,128)(2,1)S(1)}, u32[]{:S(2)}) copy-start(bf16[2,128,256]{2,1,0:T(8,128)(2,1)S(1)} %collective-permute-done.7.refs_7_) | copy-start | bytes 393220
  45.3 5.5 %collective-permute-start.11 = (bf16[8,32,128]{2,1,0:T(8,128)(2,1)}, bf16[8,32,128]{2,1,0:T(8,128)(2,1)S(1)}, u32[]{:S(2)}, u32[]{:S(2)}) collective-permute-start(bf16[8,32,128]{2,1,0:T(8,128)(2,1)} %get-tuple-element.10), channel_id=1, source_target_pairs={{0,1},{1,2},{2,3},{3,0},{4,5},{5,6},{6,7},{7,4},{8,9},{9,10},{10,1... | collective-permute-start | bytes 196616 | tf_op jit(solution)/shard_map/ppermute | solution.py:131
  45.9 6.0 %collective-permute-start.12 = (bf16[8,32,128]{2,1,0:T(8,128)(2,1)}, bf16[8,32,128]{2,1,0:T(8,128)(2,1)S(1)}, u32[]{:S(2)}, u32[]{:S(2)}) collective-permute-start(bf16[8,32,128]{2,1,0:T(8,128)(2,1)} %get-tuple-element.11), channel_id=1, source_target_pairs={{0,2},{1,3},{2,0},{3,1},{4,6},{5,7},{6,4},{7,5},{8,10},{9,11},{10,... | collective-permute-start | bytes 196616 | tf_op jit(solution)/shard_map/ppermute | solution.py:131
  47.9 5.5 %collective-permute-start.13 = (bf16[8,32,128]{2,1,0:T(8,128)(2,1)}, bf16[8,32,128]{2,1,0:T(8,128)(2,1)S(1)}, u32[]{:S(2)}, u32[]{:S(2)}) collective-permute-start(bf16[8,32,128]{2,1,0:T(8,128)(2,1)} %get-tuple-element.12), channel_id=1, source_target_pairs={{0,3},{1,0},{2,1},{3,2},{4,7},{5,4},{6,5},{7,6},{8,11},{9,8},{10,9... | collective-permute-start | bytes 196616 | tf_op jit(solution)/shard_map/ppermute | solution.py:131
  50.8 2.6 %copy-start.11 = (bf16[8,32,128]{2,1,0:T(8,128)(2,1)}, bf16[8,32,128]{2,1,0:T(8,128)(2,1)S(1)}, u32[]{:S(2)}) copy-start(bf16[8,32,128]{2,1,0:T(8,128)(2,1)S(1)} %collective-permute-done.11.refs_0_) | copy-start | bytes 196612
  51.9 1.5 %copy-start.12 = (bf16[8,32,128]{2,1,0:T(8,128)(2,1)}, bf16[8,32,128]{2,1,0:T(8,128)(2,1)S(1)}, u32[]{:S(2)}) copy-start(bf16[8,32,128]{2,1,0:T(8,128)(2,1)S(1)} %collective-permute-done.12.refs_1_) | copy-start | bytes 196612
  53.4 0.6 %copy-start.13 = (bf16[8,32,128]{2,1,0:T(8,128)(2,1)}, bf16[8,32,128]{2,1,0:T(8,128)(2,1)S(1)}, u32[]{:S(2)}) copy-start(bf16[8,32,128]{2,1,0:T(8,128)(2,1)S(1)} %collective-permute-done.13.refs_2_) | copy-start | bytes 196612

commit v2 on v0

v2 whole, which is shorter than its diff:
```python
from functools import partial

import jax
import jax.numpy as jnp
from jax import lax
from jax.experimental import pallas as pl
from jax.experimental.pallas import tpu as pltpu
from jax.sharding import PartitionSpec as P


KS_DEV = 8
N_ACC = 4
SHIFT = 16
BIG = 1 << SHIFT
VMEM = pl.BlockSpec(memory_space=pltpu.VMEM)
SMEM = pl.BlockSpec(memory_space=pltpu.SMEM)
HBM = pl.BlockSpec(memory_space=pltpu.HBM)
F32 = jnp.float32
BF16 = jnp.bfloat16


def in_hbm(x):
    return pltpu.with_memory_space_constraint(x, pltpu.HBM)


def iota(shape, axis):
    return lax.broadcasted_iota(jnp.int32, shape, axis)


def partner(i, d, n):
    return i ^ d if n & (n - 1) == 0 else (n - i + d) % n


def step_of(q, n):
    return (q + n - 1) % n


def unroll_of(count, most):
    return max(u for u in range(1, most + 1) if count % u == 0)


def left_kernel(n_cols, fan, agg_blocks, rows_hbm, cols_hbm, piece_hbm, *refs):
    got, rest = refs[: n_cols - 1], refs[n_cols - 1 :]
    blocks_hbm, left_ref, table_ref, turned, own, blocks_ref, rows_ref, cols_ref = rest[:8]
    block_sems, own_sem, row_sem, col_sem = rest[8:]
    parts = (own,) + got
    per_part, node, width = own.shape
    count = blocks_ref.shape[0]
    n_chunks = block_sems.shape[0]
    size = count // n_chunks
    chunks = [
        pltpu.make_async_copy(
            blocks_hbm.at[pl.ds(c * size, size)], blocks_ref.at[pl.ds(c * size, size)], block_sems.at[c]
        )
        for c in range(n_chunks)
    ]
    get_rows = pltpu.make_async_copy(rows_hbm, rows_ref, row_sem)
    get_cols = pltpu.make_async_copy(cols_hbm, cols_ref, col_sem)
    get_own = pltpu.make_async_copy(piece_hbm, own, own_sem)
    get_rows.start()
    get_cols.start()
    get_own.start()
    for chunk in chunks:
        chunk.start()

    agg = width // agg_blocks
    half = agg // 2
    tall = agg_blocks * half
    out_row, in_col = iota((width, width), 0), iota((width, width), 1)
    within = out_row % tall
    wanted = (within // half) * agg + 2 * (within % half) + out_row // tall
    order = jnp.where(in_col == wanted, 1.0, 0.0).astype(BF16)
    me = lax.axis_index("col")
    for step in list(range(1, n_cols)) + [0]:
        if step == 0:
            get_own.wait()
        source = lax.rem(me - step + n_cols, n_cols)
        for e in range(per_part):
            turned[source * per_part + e] = lax.dot_general(
                order, parts[step][e], (((1,), (1,)), ((), ())), preferred_element_type=F32
            ).astype(BF16)

    get_rows.wait()
    get_cols.wait()
    row = lax.axis_index("row")
    mine, line = lax.rem(row, fan), lax.div(row, fan)
    table_ref[count] = 0

    def enter(k, n):
        j = cols_ref[k]
        e, source, owner = lax.rem(j, per_part), lax.rem(lax.div(j, per_part), n_cols), lax.div(j, n_cols * per_part)
        q = lax.rem(line - source + n_cols + 1, n_cols)
        g = lax.rem(mine - owner + fan, fan)
        early = (g == 0) & (q < n_cols - 1)
        part = jnp.where(early, q, jnp.where(g == 0, 0, 1 + (g - 1) * n_cols + q))
        place = jnp.where(early, n, count - 1 - (k - n))
        table_ref[place] = k + (part * per_part + e + 1) * BIG
        return n + jnp.where(early, 1, 0)

    unroll = unroll_of(size, 8)

    def some(b, n):
        for u in range(unroll):
            k = b * unroll + u
            both = jnp.dot(turned[rows_ref[k]], blocks_ref[k], preferred_element_type=F32).astype(BF16)
            left_ref[k, :, :node] = both[:tall]
            left_ref[k, :, node:] = both[tall:]
            n = enter(k, n)
        return n

    n = jnp.int32(0)
    for c, chunk in enumerate(chunks):
        chunk.wait()
        n = lax.fori_loop(c * size // unroll, (c + 1) * size // unroll, some, n)
    table_ref[count + 1] = n


def spread(piece, agg_blocks):
    node, width = piece.shape
    agg = width // agg_blocks
    low = iota((node, 2 * agg), 1) < agg
    zero = jnp.zeros((node, 2 * agg), BF16)
    top, bottom = [], []
    for v in range(agg_blocks // 2):
        straight = piece[:, v * 2 * agg : (v + 1) * 2 * agg]
        turned = pltpu.roll(straight.astype(F32), agg, 1).astype(BF16)
        top += [jnp.where(low, straight, zero), jnp.where(low, turned, zero)]
        bottom += [jnp.where(low, zero, turned), jnp.where(low, zero, straight)]
    return top, bottom


def sum_kernel(n_parts, early, agg_blocks, unroll, table_in, slots_hbm, *refs):
    parts, left_ref, rest = refs[:n_parts], refs[n_parts], refs[n_parts + 1 :]
    before = None
    if not early:
        before, rest = rest[0], rest[1:]
    outs, rest = rest[: -6 - N_ACC], rest[-6 - N_ACC :]
    table_ref, slots_ref, table_sem, slot_sem, wide, turn = rest[:6]
    accs = rest[6:]
    count = left_ref.shape[0]
    get_slots = pltpu.make_async_copy(slots_hbm, slots_ref, slot_sem)
    get_slots.start()
    get_table = pltpu.make_async_copy(table_in, table_ref, table_sem)
    get_table.start()
    per_part, node, width = parts[0].shape
    agg = width // agg_blocks
    half = agg // 2
    lanes = 2 * agg
    for i, acc in enumerate(accs):
        acc[...] = before[...] if i == 0 and before is not None else jnp.zeros_like(acc)
    wide[0] = jnp.zeros_like(wide[0])
    for q, part in enumerate(parts):
        for e in range(per_part):
            for h, blocks in enumerate(spread(part[e], agg_blocks)):
                for s, block in enumerate(blocks):
                    wide[1 + q * per_part + e, h * node : (h + 1) * node, s * lanes : (s + 1) * lanes] = block

    get_table.wait()
    get_slots.wait()
    n = table_ref[count + 1] if early else count - table_ref[count + 1]

    def some(b, _):
        for u in range(unroll):
            p = b * unroll + u
            entry = table_ref[jnp.where(p < n, p if early else count - 1 - p, count)]
            k = entry & (BIG - 1)
            term = jnp.dot(left_ref[k], wide[lax.shift_right_logical(entry, SHIFT)], preferred_element_type=F32)
            for i in range(agg_blocks * agg_blocks):
                t, s = divmod(i, agg_blocks)
                slot = slots_ref[t, s, k]
                accs[i % N_ACC][slot] += term[t * half : (t + 1) * half, s * lanes : (s + 1) * lanes]
        return 0

    lax.fori_loop(0, lax.div(n + unroll - 1, unroll), some, 0)

    if early:
        total = accs[0][...]
        for acc in accs[1:]:
            total += acc[...]
        outs[0][...] = total
        return
    me = lax.axis_index("col")
    for step, out in enumerate(outs):
        slots = pl.ds(partner(me, step, len(outs)) * KS_DEV, KS_DEV)
        total = accs[0][slots]
        for acc in accs[1:]:
            total += acc[slots]
        turn[step] = total.reshape(KS_DEV * half, lanes)
        for a in range(half):
            out[:, a * lanes : (a + 1) * lanes] = turn[step, pl.ds(a, KS_DEV, stride=half), :].astype(out.dtype)


def on_device(a_blocks, a_rows, a_cols, p_blocks, coarse_slot):
    rows_total = lax.axis_size("row")
    cols_total = lax.axis_size("col")
    fan = rows_total // cols_total
    per_part, node, width = p_blocks.shape
    count = a_blocks.shape[2]
    agg_blocks = coarse_slot.shape[3]
    agg = width // agg_blocks

    def shift(x, to):
        return lax.ppermute(x, "col", [(i, to(i)) for i in range(cols_total)])

    def across(x, g):
        swap = [(r, (r // fan) * fan + (r % fan + g) % fan) for r in range(rows_total)]
        return lax.ppermute(x, "row", swap)

    row_parts = [p_blocks]
    for d in range(1, cols_total):
        row_parts.append(shift(p_blocks, lambda i, d=d: (i + d) % cols_total))
    direct = []
    for q in range(cols_total):
        pairs = []
        for c in range(cols_total):
            for f in range(fan):
                for x in range(cols_total):
                    target = ((x + step_of(q, cols_total)) % cols_total) * fan + f
                    pairs.append(((c * fan + f) * cols_total + x, target * cols_total + c))
        direct.append(lax.ppermute(p_blocks, ("row", "col"), pairs))
    early, late = direct[:-1], direct[-1:]
    for g in range(1, fan):
        late += [across(part, g) for part in direct]

    rows, cols = in_hbm(a_rows.reshape(-1)), in_hbm(a_cols.reshape(-1))
    slots = in_hbm(coarse_slot.transpose(0, 1, 3, 4, 2).reshape(agg_blocks, agg_blocks, count))
    table = jax.ShapeDtypeStruct((count + 2,), jnp.int32)
    left, table_in = pl.pallas_call(
        partial(left_kernel, cols_total, fan, agg_blocks),
        out_shape=[jax.ShapeDtypeStruct((count, width // 2, 2 * node), BF16), table],
        in_specs=[HBM] * 3 + [VMEM] * (cols_total - 1) + [HBM],
        out_specs=[VMEM, SMEM],
        scratch_shapes=[
            pltpu.VMEM((per_part * cols_total, width, node), BF16),
            pltpu.VMEM((per_part, node, width), BF16),
            pltpu.VMEM((count, node, node), BF16),
            pltpu.SMEM((count,), jnp.int32),
            pltpu.SMEM((count,), jnp.int32),
            pltpu.SemaphoreType.DMA((unroll_of(count, 4),)),
        ]
        + [pltpu.SemaphoreType.DMA] * 3,
        compiler_params=pltpu.CompilerParams(vmem_limit_bytes=16 << 20),
        cost_estimate=pl.CostEstimate(
            flops=2 * count * width * node * node, bytes_accessed=20 << 20, transcendentals=0
        ),
        name="left",
    )(rows, cols, in_hbm(p_blocks), *row_parts[1:], in_hbm(a_blocks.reshape(a_blocks.shape[2:])))

    chunk = (KS_DEV, agg * agg)
    block = (agg // 2, 2 * agg)
    slot_count = KS_DEV * cols_total
    sums = []
    for stage, parts in enumerate((early, late)):
        if stage:
            outs = [jax.ShapeDtypeStruct(chunk, BF16 if q else F32) for q in range(cols_total)]
        else:
            outs = [jax.ShapeDtypeStruct((slot_count,) + block, F32)]
        sums = pl.pallas_call(
            partial(sum_kernel, len(parts), not stage, agg_blocks, 12 if stage else 8),
            out_shape=outs,
            in_specs=[pl.BlockSpec(memory_space=pl.ANY), HBM] + [VMEM] * (len(parts) + 1 + stage),
            out_specs=[VMEM] * len(outs),
            scratch_shapes=[
                pltpu.SMEM(table.shape, jnp.int32),
                pltpu.SMEM((agg_blocks, agg_blocks, count), jnp.int32),
                pltpu.SemaphoreType.DMA,
                pltpu.SemaphoreType.DMA,
                pltpu.VMEM((1 + len(parts) * per_part, 2 * node, 2 * width), BF16),
                pltpu.VMEM((cols_total, KS_DEV * block[0], block[1]), F32),
            ]
            + [pltpu.VMEM((slot_count,) + block, F32)] * N_ACC,
            compiler_params=pltpu.CompilerParams(vmem_limit_bytes=36 << 20),
            cost_estimate=pl.CostEstimate(
                flops=4 * count * width * node * node, bytes_accessed=10 << 20, transcendentals=0
            ),
        )(table_in, slots, *parts, left, *sums)
    total = sums[0]
    for d in range(1, cols_total):
        total += shift(sums[d], lambda i, d=d: partner(i, d, cols_total)).astype(F32)
    return total.astype(BF16)[None]


def solution(mesh):
    placed = (
        P("row", "col", None, None, None),
        P("row", "col", None),
        P("row", "col", None),
        P(("row", "col"), None, None),
        P("row", "col", None, None, None),
    )

    return jax.shard_map(on_device, mesh=mesh, in_specs=placed, out_specs=P("row", "col", None), check_vma=False)
```

time: 315 us -> 45.3 us (0.14)
  local copies, waits for them, and re-layouts: 133 us -> 0 us
  other arithmetic: 49.7 us -> 0.66 us
  matrix products: 44 us -> 0 us
  blocking collectives: 40.7 us -> 0 us
  waiting for transfers between devices: 27.4 us -> 9.34 us
  starting transfers between devices: 3.66 us -> 21.4 us
  between operations: 14.1 us -> 0.09 us
  Pallas kernels: 0 us -> 13.6 us
    transpose x6 -> x0, local copies, waits for them, and re-layouts: 55.6 us -> none  [accumulate(): jnp.einsum('knta,knsb->ktsab', left_split, right_split, preferred_element...]
    reshape x12 -> x0, local copies, waits for them, and re-layouts: 48 us -> none  [the longest x6 47.4 us: accumulate(): contribs.reshape(group_size * agg_blocks * agg_blocks, agg_width * agg_wi...]
    scatter-add x6 -> x0, other arithmetic: 46.8 us -> none  [accumulate(): running = running.at[sls.reshape(-1)].add(contribs)]
    dot_general x12 -> x0, matrix products: 44 us -> none  [the longest x6 34.7 us: accumulate(): jnp.einsum('knta,knsb->ktsab', left_split, right_split, preferred_element...]
    all_gather x1 -> x0, waiting for transfers between devices: 26.7 us -> none  [on_device(): column_rows = lax.all_gather(p_blocks, 'row', axis=0, tiled=True)]
    unnamed x1 -> x0, blocking collectives: 26.4 us -> none
    ppermute x0 -> x14, starting transfers between devices: none -> 21.4 us  [the longest x4 11.6 us: on_device(): direct.append(lax.ppermute(p_blocks, ('row', 'col'), pairs))]
    gather x18 -> x0, local copies, waits for them, and re-layouts: 15.7 us -> none  [the longest x12 12 us: accumulate(): left_rows = jnp.take(row_panel, rws, axis=0)]
  transfers between devices with their start and end apart: 2 -> 14, of which waited for: 1 -> 5; matrix products, arithmetic and copies ran while one was open for 2% -> 0% of each run, Pallas kernels for 0% -> 19%
where the time goes in v2:
time: 45.3 us; the launch traced here: 45.1 us
  starting transfers between devices  21.4 us (47%)
  Pallas kernels  13.6 us (30%)
  waiting for transfers between devices  9.34 us (21%)
  other arithmetic  0.66 us (1%)
    ppermute x4, starting transfers between devices, on_device(): direct.append(lax.ppermute(p_blocks, ('row', 'col'), pairs))  11.6 us
    ppermute x6, starting transfers between devices, shift(): return lax.ppermute(x, 'col', [(i, to(i)) for i in range(cols_total)])  9.1 us
    pallas_call x2, Pallas kernels, on_device(): pl.pallas_call(partial(sum_kernel, len(parts), not stage, agg_blocks, 12...  7.65 us
    pallas_call x1, Pallas kernels, on_device(): pl.pallas_call(partial(left_kernel, cols_total, fan, agg_blocks), out_sha...  5.95 us
    ppermute x6, waiting for transfers between devices, shift(): return lax.ppermute(x, 'col', [(i, to(i)) for i in range(cols_total)])  5.59 us
    ppermute x4, waiting for transfers between devices, on_device(): direct.append(lax.ppermute(p_blocks, ('row', 'col'), pairs))  3.74 us
  transfers between devices with their start and end apart: 14, of which 5 were waited for; matrix products, arithmetic and copies ran while one was open for 0% of the time, Pallas kernels for 19%

profile of v2, /device:TPU:0, one launch (start us, length us, event | category | flops | bytes accessed | tf_op | source)
XLA Modules:
  0.0 45.1 jit_solution(2080667546681137701)
XLA Ops:
  0.0 3.0 %collective-permute-start = (bf16[2,128,256]{2,1,0:T(8,128)(2,1)}, bf16[2,128,256]{2,1,0:T(8,128)(2,1)S(1)}, u32[]{:S(2)}, u32[]{:S(2)}) collective-permute-start(bf16[2,128,256]{2,1,0:T(8,128)(2,1)} %piece_hbm.1), channel_id=1, source_target_pairs={{0,1},{1,2},{2,3},{3,0},{4,5},{5,6},{6,7},{7,4},{8,9},{9,10},{10,1... | collective-permute-start | bytes 393224 | tf_op jit(solution)/shard_map/ppermute | solution.py:203
  3.0 1.5 %collective-permute-start.1 = (bf16[2,128,256]{2,1,0:T(8,128)(2,1)}, bf16[2,128,256]{2,1,0:T(8,128)(2,1)S(1)}, u32[]{:S(2)}, u32[]{:S(2)}) collective-permute-start(bf16[2,128,256]{2,1,0:T(8,128)(2,1)} %piece_hbm.1), channel_id=1, source_target_pairs={{0,2},{1,3},{2,0},{3,1},{4,6},{5,7},{6,4},{7,5},{8,10},{9,11},{10,... | collective-permute-start | bytes 393224 | tf_op jit(solution)/shard_map/ppermute | solution.py:203
  4.5 2.6 %collective-permute-start.3 = (bf16[2,128,256]{2,1,0:T(8,128)(2,1)}, bf16[2,128,256]{2,1,0:T(8,128)(2,1)S(1)}, u32[]{:S(2)}, u32[]{:S(2)}) collective-permute-start(bf16[2,128,256]{2,1,0:T(8,128)(2,1)} %piece_hbm.1), channel_id=1, source_target_pairs={{0,16},{1,24},{2,0},{3,8},{4,20},{5,28},{6,4},{7,12},{8,17},{9,25}... | collective-permute-start | bytes 393224 | tf_op jit(solution)/shard_map/ppermute | solution.py:220
  7.1 2.3 %collective-permute-start.4 = (bf16[2,128,256]{2,1,0:T(8,128)(2,1)}, bf16[2,128,256]{2,1,0:T(8,128)(2,1)S(1)}, u32[]{:S(2)}, u32[]{:S(2)}) collective-permute-start(bf16[2,128,256]{2,1,0:T(8,128)(2,1)} %piece_hbm.1), channel_id=1, source_target_pairs={{0,24},{1,0},{2,8},{3,16},{4,28},{5,4},{6,12},{7,20},{8,25},{9,1},... | collective-permute-start | bytes 393224 | tf_op jit(solution)/shard_map/ppermute | solution.py:220
  9.4 1.6 %collective-permute-start.6 = (bf16[2,128,256]{2,1,0:T(8,128)(2,1)}, bf16[2,128,256]{2,1,0:T(8,128)(2,1)S(1)}, u32[]{:S(2)}, u32[]{:S(2)}) collective-permute-start(bf16[2,128,256]{2,1,0:T(8,128)(2,1)} %piece_hbm.1), channel_id=1, source_target_pairs={{0,0},{1,8},{2,16},{3,24},{4,4},{5,12},{6,20},{7,28},{8,1},{9,9},{... | collective-permute-start | bytes 393224 | tf_op jit(solution)/shard_map/ppermute | solution.py:220
  11.0 0.0 collective-permute-done.refs_0_
  11.0 5.2 %collective-permute-start.8 = (bf16[2,128,256]{2,1,0:T(8,128)(2,1)}, bf16[2,128,256]{2,1,0:T(8,128)(2,1)S(1)}, u32[]{:S(2)}, u32[]{:S(2)}) collective-permute-start(bf16[2,128,256]{2,1,0:T(8,128)(2,1)} %piece_hbm.1), channel_id=1, source_target_pairs={{0,8},{1,16},{2,24},{3,0},{4,12},{5,20},{6,28},{7,4},{8,9},{9,17},... | collective-permute-start | bytes 393224 | tf_op jit(solution)/shard_map/ppermute | solution.py:220
  16.1 0.0 collective-permute-done.1.refs_1_
  16.1 0.0 collective-permute-start.2
  16.1 0.0 collective-permute-done.3.refs_0_
  16.1 0.1 collective-permute-start.10
  16.2 0.0 collective-permute-done.4.refs_0_
  16.2 0.5 %collective-permute-start.5 = (bf16[2,128,256]{2,1,0:T(8,128)(2,1)S(1)}, bf16[2,128,256]{2,1,0:T(8,128)(2,1)S(1)}, u32[]{:S(2)}, u32[]{:S(2)}) collective-permute-start(bf16[2,128,256]{2,1,0:T(8,128)(2,1)S(1)} %collective-permute-done.4.refs_0_), channel_id=1, source_target_pairs={{0,4},{4,0},{8,12},{12,8},{16,20},{20,16},{24,28},{28,24},{1,5},{5... | collective-permute-start | bytes 393224 | tf_op jit(solution)/shard_map/ppermute | solution.py:207
  16.7 0.0 collective-permute-done.6.refs_1_
  16.7 0.1 collective-permute-start.7
  16.8 3.7 %collective-permute-done.8.refs_2_ = bf16[2,128,256]{2,1,0:T(8,128)(2,1)S(1)} collective-permute-done((bf16[2,128,256]{2,1,0:T(8,128)(2,1)}, bf16[2,128,256]{2,1,0:T(8,128)(2,1)S(1)}, u32[]{:S(2)}, u32[]{:S(2)}) %collective-permute-start.8) | collective-permute-done | bytes 131104 | tf_op jit(solution)/shard_map/ppermute | solution.py:220
  20.5 0.0 collective-permute-start.9
  20.5 0.8 %collective-permute-done.2.refs_2_ = bf16[2,128,256]{2,1,0:T(8,128)(2,1)S(1)} collective-permute-done((bf16[2,128,256]{2,1,0:T(8,128)(2,1)}, bf16[2,128,256]{2,1,0:T(8,128)(2,1)S(1)}, u32[]{:S(2)}, u32[]{:S(2)}) %collective-permute-start.2) | collective-permute-done | bytes 131104 | tf_op jit(solution)/shard_map/ppermute | solution.py:203
  21.4 5.9 %left.1 = (bf16[96,128,256]{2,1,0:T(8,128)(2,1)S(1)}, s32[98]{0:T(128)S(1)}) custom-call(s32[96]{0:T(128)} %bitcast.11, s32[96]{0:T(128)} %bitcast.12, bf16[2,128,256]{2,1,0:T(8,128)(2,1)} %piece_hbm.1, bf16[2,128,256]{2,1,0:T(8,128)(2,1)S(1)} %collective-permute-done.refs_0_, bf16[2,128,256]{2,1,0:T(8,128)(2,1)S(1)} %collective-permute-done.1.refs_1_, ...), custom_call_target="tpu_custom_call" | custom-call | flops 805306368 | bytes 20971520 | tf_op jit(solution)/shard_map/left/pallas_call | solution.py:228
  27.3 2.8 %shard_map.55.refs_6_ = f32[32,32,128]{2,1,0:T(8,128)S(1)} custom-call(s32[98]{0:T(128)S(1)} %get-tuple-element.11.table_in, s32[4,4,96]{2,1,0:T(4,128)} %bitcast.9, bf16[2,128,256]{2,1,0:T(8,128)(2,1)S(1)} %collective-permute-done.4.refs_0_, bf16[2,128,256]{2,1,0:T(8,128)(2,1)S(1)} %collective-permute-done.6.refs_1_, ...), custom_call_target="tpu_custom_call" | custom-call | flops 1610612736 | bytes 10485760 | tf_op jit(solution)/shard_map/pallas_call | solution.py:258
  30.1 0.0 collective-permute-done.10.refs_4_
  30.1 0.0 collective-permute-done.5.refs_1_
  30.1 0.0 collective-permute-done.7.refs_2_
  30.1 0.0 collective-permute-done.9.refs_3_
  30.1 4.9 %shard_map.56 = (f32[8,4096]{1,0:T(8,128)S(1)}, bf16[8,4096]{1,0:T(8,128)(2,1)S(1)}, bf16[8,4096]{1,0:T(8,128)(2,1)S(1)}, bf16[8,4096]{1,0:T(8,128)(2,1)S(1)}) custom-call(s32[98]{0:T(128)S(1)} %get-tuple-element.11.table_in, s32[4,4,96]{2,1,0:T(4,128)} %bitcast.10, bf16[2,128,256]{2,1,0:T(8,128)(2,1)S(1)} %collective-permute-done.3.refs_0_, ...), custom_call_target="tpu_custom_call" | custom-call | flops 1610612736 | bytes 10485760 | tf_op jit(solution)/shard_map/pallas_call | solution.py:258
  35.0 2.6 %collective-permute-start.11 = (bf16[8,4096]{1,0:T(8,128)(2,1)S(1)}, bf16[8,4096]{1,0:T(8,128)(2,1)S(1)}, u32[]{:S(2)}, u32[]{:S(2)}) collective-permute-start(bf16[8,4096]{1,0:T(8,128)(2,1)S(1)} %get-tuple-element.14), channel_id=1, source_target_pairs={{0,1},{1,0},{2,3},{3,2},{4,5},{5,4},{6,7},{7,6},{8,9},{9,8},{10,11... | collective-permute-start | bytes 196616 | tf_op jit(solution)/shard_map/ppermute | solution.py:203
  37.7 1.6 %collective-permute-start.12 = (bf16[8,4096]{1,0:T(8,128)(2,1)S(1)}, bf16[8,4096]{1,0:T(8,128)(2,1)S(1)}, u32[]{:S(2)}, u32[]{:S(2)}) collective-permute-start(bf16[8,4096]{1,0:T(8,128)(2,1)S(1)} %get-tuple-element.15), channel_id=1, source_target_pairs={{0,2},{1,3},{2,0},{3,1},{4,6},{5,7},{6,4},{7,5},{8,10},{9,11},{10,... | collective-permute-start | bytes 196616 | tf_op jit(solution)/shard_map/ppermute | solution.py:203
  39.2 0.4 collective-permute-start.13
  39.6 0.5 %collective-permute-done.11 = bf16[8,4096]{1,0:T(8,128)(2,1)S(1)} collective-permute-done((bf16[8,4096]{1,0:T(8,128)(2,1)S(1)}, bf16[8,4096]{1,0:T(8,128)(2,1)S(1)}, u32[]{:S(2)}, u32[]{:S(2)}) %collective-permute-start.11) | collective-permute-done | bytes 65568 | tf_op jit(solution)/shard_map/ppermute | solution.py:203
  40.2 3.0 %collective-permute-done.12 = bf16[8,4096]{1,0:T(8,128)(2,1)S(1)} collective-permute-done((bf16[8,4096]{1,0:T(8,128)(2,1)S(1)}, bf16[8,4096]{1,0:T(8,128)(2,1)S(1)}, u32[]{:S(2)}, u32[]{:S(2)}) %collective-permute-start.12) | collective-permute-done | bytes 65568 | tf_op jit(solution)/shard_map/ppermute | solution.py:203
  43.2 1.2 %collective-permute-done.13 = bf16[8,4096]{1,0:T(8,128)(2,1)S(1)} collective-permute-done((bf16[8,4096]{1,0:T(8,128)(2,1)S(1)}, bf16[8,4096]{1,0:T(8,128)(2,1)S(1)}, u32[]{:S(2)}, u32[]{:S(2)}) %collective-permute-start.13) | collective-permute-done | bytes 65568 | tf_op jit(solution)/shard_map/ppermute | solution.py:203
  44.4 0.7 %fusion = bf16[1,8,4096]{2,1,0:T(8,128)(2,1)} fusion(bf16[8,4096]{1,0:T(8,128)(2,1)S(1)} %collective-permute-done.13, bf16[8,4096]{1,0:T(8,128)(2,1)S(1)} %collective-permute-done.12, f32[8,4096]{1,0:T(8,128)S(1)} %get-tuple-element.13, bf16[8,4096]{1,0:T(8,128)(2,1)S(1)} %collective-permute-done.11), kind=kLoop, calls=%fused_computation.1 | loop fusion | flops 229376 | bytes 393216 | tf_op jit(solution)/shard_map/broadcast_in_dim | solution.py:280
Async XLA Ops:
  0.0 11.0 %collective-permute-start = (bf16[2,128,256]{2,1,0:T(8,128)(2,1)}, bf16[2,128,256]{2,1,0:T(8,128)(2,1)S(1)}, u32[]{:S(2)}, u32[]{:S(2)}) collective-permute-start(bf16[2,128,256]{2,1,0:T(8,128)(2,1)} %piece_hbm.1), channel_id=1, source_target_pairs={{0,1},{1,2},{2,3},{3,0},{4,5},{5,6},{6,7},{7,4},{8,9},{9,10},{10,1... | collective-permute-start | bytes 393224 | tf_op jit(solution)/shard_map/ppermute | solution.py:203
  3.0 13.2 %collective-permute-start.1 = (bf16[2,128,256]{2,1,0:T(8,128)(2,1)}, bf16[2,128,256]{2,1,0:T(8,128)(2,1)S(1)}, u32[]{:S(2)}, u32[]{:S(2)}) collective-permute-start(bf16[2,128,256]{2,1,0:T(8,128)(2,1)} %piece_hbm.1), channel_id=1, source_target_pairs={{0,2},{1,3},{2,0},{3,1},{4,6},{5,7},{6,4},{7,5},{8,10},{9,11},{10,... | collective-permute-start | bytes 393224 | tf_op jit(solution)/shard_map/ppermute | solution.py:203
  4.5 11.6 %collective-permute-start.3 = (bf16[2,128,256]{2,1,0:T(8,128)(2,1)}, bf16[2,128,256]{2,1,0:T(8,128)(2,1)S(1)}, u32[]{:S(2)}, u32[]{:S(2)}) collective-permute-start(bf16[2,128,256]{2,1,0:T(8,128)(2,1)} %piece_hbm.1), channel_id=1, source_target_pairs={{0,16},{1,24},{2,0},{3,8},{4,20},{5,28},{6,4},{7,12},{8,17},{9,25}... | collective-permute-start | bytes 393224 | tf_op jit(solution)/shard_map/ppermute | solution.py:220
  7.1 9.1 %collective-permute-start.4 = (bf16[2,128,256]{2,1,0:T(8,128)(2,1)}, bf16[2,128,256]{2,1,0:T(8,128)(2,1)S(1)}, u32[]{:S(2)}, u32[]{:S(2)}) collective-permute-start(bf16[2,128,256]{2,1,0:T(8,128)(2,1)} %piece_hbm.1), channel_id=1, source_target_pairs={{0,24},{1,0},{2,8},{3,16},{4,28},{5,4},{6,12},{7,20},{8,25},{9,1},... | collective-permute-start | bytes 393224 | tf_op jit(solution)/shard_map/ppermute | solution.py:220
  9.4 7.3 %collective-permute-start.6 = (bf16[2,128,256]{2,1,0:T(8,128)(2,1)}, bf16[2,128,256]{2,1,0:T(8,128)(2,1)S(1)}, u32[]{:S(2)}, u32[]{:S(2)}) collective-permute-start(bf16[2,128,256]{2,1,0:T(8,128)(2,1)} %piece_hbm.1), channel_id=1, source_target_pairs={{0,0},{1,8},{2,16},{3,24},{4,4},{5,12},{6,20},{7,28},{8,1},{9,9},{... | collective-permute-start | bytes 393224 | tf_op jit(solution)/shard_map/ppermute | solution.py:220
  11.0 9.6 %collective-permute-start.8 = (bf16[2,128,256]{2,1,0:T(8,128)(2,1)}, bf16[2,128,256]{2,1,0:T(8,128)(2,1)S(1)}, u32[]{:S(2)}, u32[]{:S(2)}) collective-permute-start(bf16[2,128,256]{2,1,0:T(8,128)(2,1)} %piece_hbm.1), channel_id=1, source_target_pairs={{0,8},{1,16},{2,24},{3,0},{4,12},{5,20},{6,28},{7,4},{8,9},{9,17},... | collective-permute-start | bytes 393224 | tf_op jit(solution)/shard_map/ppermute | solution.py:220
  16.1 5.2 %collective-permute-start.2 = (bf16[2,128,256]{2,1,0:T(8,128)(2,1)}, bf16[2,128,256]{2,1,0:T(8,128)(2,1)S(1)}, u32[]{:S(2)}, u32[]{:S(2)}) collective-permute-start(bf16[2,128,256]{2,1,0:T(8,128)(2,1)} %piece_hbm.1), channel_id=1, source_target_pairs={{0,3},{1,0},{2,1},{3,2},{4,7},{5,4},{6,5},{7,6},{8,11},{9,8},{10,9... | collective-permute-start | bytes 393224 | tf_op jit(solution)/shard_map/ppermute | solution.py:203
  16.1 14.0 %collective-permute-start.10 = (bf16[2,128,256]{2,1,0:T(8,128)(2,1)S(1)}, bf16[2,128,256]{2,1,0:T(8,128)(2,1)S(1)}, u32[]{:S(2)}, u32[]{:S(2)}) collective-permute-start(bf16[2,128,256]{2,1,0:T(8,128)(2,1)S(1)} %collective-permute-done.3.refs_0_), channel_id=1, source_target_pairs={{0,4},{4,0},{8,12},{12,8},{16,20},{20,16},{24,28},{28,24},{1,5},{5... | collective-permute-start | bytes 393224 | tf_op jit(solution)/shard_map/ppermute | solution.py:207
  16.2 13.9 %collective-permute-start.5 = (bf16[2,128,256]{2,1,0:T(8,128)(2,1)S(1)}, bf16[2,128,256]{2,1,0:T(8,128)(2,1)S(1)}, u32[]{:S(2)}, u32[]{:S(2)}) collective-permute-start(bf16[2,128,256]{2,1,0:T(8,128)(2,1)S(1)} %collective-permute-done.4.refs_0_), channel_id=1, source_target_pairs={{0,4},{4,0},{8,12},{12,8},{16,20},{20,16},{24,28},{28,24},{1,5},{5... | collective-permute-start | bytes 393224 | tf_op jit(solution)/shard_map/ppermute | solution.py:207
  16.7 13.4 %collective-permute-start.7 = (bf16[2,128,256]{2,1,0:T(8,128)(2,1)S(1)}, bf16[2,128,256]{2,1,0:T(8,128)(2,1)S(1)}, u32[]{:S(2)}, u32[]{:S(2)}) collective-permute-start(bf16[2,128,256]{2,1,0:T(8,128)(2,1)S(1)} %collective-permute-done.6.refs_1_), channel_id=1, source_target_pairs={{0,4},{4,0},{8,12},{12,8},{16,20},{20,16},{24,28},{28,24},{1,5},{5... | collective-permute-start | bytes 393224 | tf_op jit(solution)/shard_map/ppermute | solution.py:207
  20.5 9.6 %collective-permute-start.9 = (bf16[2,128,256]{2,1,0:T(8,128)(2,1)S(1)}, bf16[2,128,256]{2,1,0:T(8,128)(2,1)S(1)}, u32[]{:S(2)}, u32[]{:S(2)}) collective-permute-start(bf16[2,128,256]{2,1,0:T(8,128)(2,1)S(1)} %collective-permute-done.8.refs_2_), channel_id=1, source_target_pairs={{0,4},{4,0},{8,12},{12,8},{16,20},{20,16},{24,28},{28,24},{1,5},{5... | collective-permute-start | bytes 393224 | tf_op jit(solution)/shard_map/ppermute | solution.py:207
  35.0 5.2 %collective-permute-start.11 = (bf16[8,4096]{1,0:T(8,128)(2,1)S(1)}, bf16[8,4096]{1,0:T(8,128)(2,1)S(1)}, u32[]{:S(2)}, u32[]{:S(2)}) collective-permute-start(bf16[8,4096]{1,0:T(8,128)(2,1)S(1)} %get-tuple-element.14), channel_id=1, source_target_pairs={{0,1},{1,0},{2,3},{3,2},{4,5},{5,4},{6,7},{7,6},{8,9},{9,8},{10,11... | collective-permute-start | bytes 196616 | tf_op jit(solution)/shard_map/ppermute | solution.py:203
  37.7 5.5 %collective-permute-start.12 = (bf16[8,4096]{1,0:T(8,128)(2,1)S(1)}, bf16[8,4096]{1,0:T(8,128)(2,1)S(1)}, u32[]{:S(2)}, u32[]{:S(2)}) collective-permute-start(bf16[8,4096]{1,0:T(8,128)(2,1)S(1)} %get-tuple-element.15), channel_id=1, source_target_pairs={{0,2},{1,3},{2,0},{3,1},{4,6},{5,7},{6,4},{7,5},{8,10},{9,11},{10,... | collective-permute-start | bytes 196616 | tf_op jit(solution)/shard_map/ppermute | solution.py:203
  39.2 5.2 %collective-permute-start.13 = (bf16[8,4096]{1,0:T(8,128)(2,1)S(1)}, bf16[8,4096]{1,0:T(8,128)(2,1)S(1)}, u32[]{:S(2)}, u32[]{:S(2)}) collective-permute-start(bf16[8,4096]{1,0:T(8,128)(2,1)S(1)} %get-tuple-element.16), channel_id=1, source_target_pairs={{0,3},{1,2},{2,1},{3,0},{4,7},{5,6},{6,5},{7,4},{8,11},{9,10},{10,... | collective-permute-start | bytes 196616 | tf_op jit(solution)/shard_map/ppermute | solution.py:203

commit v3 on v2

--- a/solution.py
+++ b/solution.py
@@ -31,37 +31,32 @@
     return i ^ d if n & (n - 1) == 0 else (n - i + d) % n
 
 
-def step_of(q, n):
-    return (q + n - 1) % n
+def hop(x, d, n):
+    return x ^ d if n & (n - 1) == 0 else (2 * n - x + d) % n
 
 
 def unroll_of(count, most):
     return max(u for u in range(1, most + 1) if count % u == 0)
 
 
+def stage_kernel(blocks_hbm, blocks_ref, sem):
+    copy = pltpu.make_async_copy(blocks_hbm, blocks_ref, sem)
+    copy.start()
+    copy.wait()
+
+
 def left_kernel(n_cols, fan, agg_blocks, rows_hbm, cols_hbm, piece_hbm, *refs):
     got, rest = refs[: n_cols - 1], refs[n_cols - 1 :]
-    blocks_hbm, left_ref, table_ref, turned, own, blocks_ref, rows_ref, cols_ref = rest[:8]
-    block_sems, own_sem, row_sem, col_sem = rest[8:]
+    blocks_ref, left_ref, table_ref, turned, own, rows_ref, cols_ref, own_sem, row_sem, col_sem = rest
     parts = (own,) + got
     per_part, node, width = own.shape
     count = blocks_ref.shape[0]
-    n_chunks = block_sems.shape[0]
-    size = count // n_chunks
-    chunks = [
-        pltpu.make_async_copy(
-            blocks_hbm.at[pl.ds(c * size, size)], blocks_ref.at[pl.ds(c * size, size)], block_sems.at[c]
-        )
-        for c in range(n_chunks)
-    ]
     get_rows = pltpu.make_async_copy(rows_hbm, rows_ref, row_sem)
+    get_own = pltpu.make_async_copy(piece_hbm, own, own_sem)
     get_cols = pltpu.make_async_copy(cols_hbm, cols_ref, col_sem)
-    get_own = pltpu.make_async_copy(piece_hbm, own, own_sem)
     get_rows.start()
     get_cols.start()
     get_own.start()
-    for chunk in chunks:
-        chunk.start()
 
     agg = width // agg_blocks
     half = agg // 2
@@ -81,38 +76,31 @@
             ).astype(BF16)
 
     get_rows.wait()
-    get_cols.wait()
     row = lax.axis_index("row")
     mine, line = lax.rem(row, fan), lax.div(row, fan)
+    steps = n_cols // fan
     table_ref[count] = 0
+    get_cols.wait()
 
     def enter(k, n):
         j = cols_ref[k]
         e, source, owner = lax.rem(j, per_part), lax.rem(lax.div(j, per_part), n_cols), lax.div(j, n_cols * per_part)
-        q = lax.rem(line - source + n_cols + 1, n_cols)
-        g = lax.rem(mine - owner + fan, fan)
-        early = (g == 0) & (q < n_cols - 1)
-        part = jnp.where(early, q, jnp.where(g == 0, 0, 1 + (g - 1) * n_cols + q))
-        place = jnp.where(early, n, count - 1 - (k - n))
-        table_ref[place] = k + (part * per_part + e + 1) * BIG
+        away = hop(source, line, n_cols) if n_cols & (n_cols - 1) == 0 else lax.rem(source + line, n_cols)
+        via, q = lax.div(away, steps), steps - 1 - lax.rem(away, steps)
+        g = lax.rem(mine - via + fan, fan)
+        early = q < (steps + 1) // 2
+        part = jnp.where(early, q, q - (steps + 1) // 2) * fan + g
+        spot = (part * fan + lax.rem(via - owner + fan, fan)) * per_part + e
+        table_ref[jnp.where(early, n, count - 1 - (k - n))] = k + (spot + 1) * BIG
         return n + jnp.where(early, 1, 0)
 
-    unroll = unroll_of(size, 8)
-
-    def some(b, n):
-        for u in range(unroll):
-            k = b * unroll + u
-            both = jnp.dot(turned[rows_ref[k]], blocks_ref[k], preferred_element_type=F32).astype(BF16)
-            left_ref[k, :, :node] = both[:tall]
-            left_ref[k, :, node:] = both[tall:]
-            n = enter(k, n)
-        return n
-
-    n = jnp.int32(0)
-    for c, chunk in enumerate(chunks):
-        chunk.wait()
-        n = lax.fori_loop(c * size // unroll, (c + 1) * size // unroll, some, n)
-    table_ref[count + 1] = n
+    def one(k, n):
+        both = jnp.dot(turned[rows_ref[k]], blocks_ref[k], preferred_element_type=F32).astype(BF16)
+        left_ref[k, :, :node] = both[:tall]
+        left_ref[k, :, node:] = both[tall:]
+        return enter(k, n)
+
+    table_ref[count + 1] = lax.fori_loop(0, count, one, jnp.int32(0), unroll=unroll_of(count, 16))
 
 
 def spread(piece, agg_blocks):
@@ -209,54 +197,65 @@
     row_parts = [p_blocks]
     for d in range(1, cols_total):
         row_parts.append(shift(p_blocks, lambda i, d=d: (i + d) % cols_total))
-    direct = []
-    for q in range(cols_total):
+    chip = jnp.concatenate([p_blocks] + [across(p_blocks, g) for g in range(1, fan)])
+    steps = cols_total // fan
+    stages = ([], [])
+    for q in range(steps):
         pairs = []
         for c in range(cols_total):
             for f in range(fan):
                 for x in range(cols_total):
-                    target = ((x + step_of(q, cols_total)) % cols_total) * fan + f
+                    target = hop(x, steps - 1 - q + steps * f, cols_total) * fan + f
                     pairs.append(((c * fan + f) * cols_total + x, target * cols_total + c))
-        direct.append(lax.ppermute(p_blocks, ("row", "col"), pairs))
-    early, late = direct[:-1], direct[-1:]
-    for g in range(1, fan):
-        late += [across(part, g) for part in direct]
+        part = lax.ppermute(chip, ("row", "col"), pairs)
+        stages[q >= (steps + 1) // 2].extend([part] + [across(part, g) for g in range(1, fan)])
 
     rows, cols = in_hbm(a_rows.reshape(-1)), in_hbm(a_cols.reshape(-1))
     slots = in_hbm(coarse_slot.transpose(0, 1, 3, 4, 2).reshape(agg_blocks, agg_blocks, count))
     table = jax.ShapeDtypeStruct((count + 2,), jnp.int32)
+    blocks = jax.ShapeDtypeStruct((count, node, node), BF16)
+    staged = pl.pallas_call(
+        stage_kernel,
+        out_shape=blocks,
+        in_specs=[HBM],
+        out_specs=VMEM,
+        scratch_shapes=[pltpu.SemaphoreType.DMA],
+        compiler_params=pltpu.CompilerParams(vmem_limit_bytes=16 << 20),
+        cost_estimate=pl.CostEstimate(flops=0, bytes_accessed=8 << 20, transcendentals=0),
+        name="stage",
+    )(in_hbm(a_blocks.reshape(blocks.shape)))
     left, table_in = pl.pallas_call(
         partial(left_kernel, cols_total, fan, agg_blocks),
         out_shape=[jax.ShapeDtypeStruct((count, width // 2, 2 * node), BF16), table],
-        in_specs=[HBM] * 3 + [VMEM] * (cols_total - 1) + [HBM],
+        in_specs=[HBM] * 3 + [VMEM] * cols_total,
         out_specs=[VMEM, SMEM],
         scratch_shapes=[
             pltpu.VMEM((per_part * cols_total, width, node), BF16),
             pltpu.VMEM((per_part, node, width), BF16),
-            pltpu.VMEM((count, node, node), BF16),
             pltpu.SMEM((count,), jnp.int32),
             pltpu.SMEM((count,), jnp.int32),
-            pltpu.SemaphoreType.DMA((unroll_of(count, 4),)),
-        ]
-        + [pltpu.SemaphoreType.DMA] * 3,
+            pltpu.SemaphoreType.DMA,
+            pltpu.SemaphoreType.DMA,
+            pltpu.SemaphoreType.DMA,
+        ],
         compiler_params=pltpu.CompilerParams(vmem_limit_bytes=16 << 20),
         cost_estimate=pl.CostEstimate(
-            flops=2 * count * width * node * node, bytes_accessed=20 << 20, transcendentals=0
+            flops=2 * count * width * node * node, bytes_accessed=10 << 20, transcendentals=0
         ),
         name="left",
-    )(rows, cols, in_hbm(p_blocks), *row_parts[1:], in_hbm(a_blocks.reshape(a_blocks.shape[2:])))
+    )(rows, cols, in_hbm(p_blocks), *row_parts[1:], staged)
 
     chunk = (KS_DEV, agg * agg)
     block = (agg // 2, 2 * agg)
     slot_count = KS_DEV * cols_total
     sums = []
-    for stage, parts in enumerate((early, late)):
+    for stage, parts in enumerate(stages):
         if stage:
             outs = [jax.ShapeDtypeStruct(chunk, BF16 if q else F32) for q in range(cols_total)]
         else:
             outs = [jax.ShapeDtypeStruct((slot_count,) + block, F32)]
         sums = pl.pallas_call(
-            partial(sum_kernel, len(parts), not stage, agg_blocks, 12 if stage else 8),
+            partial(sum_kernel, len(parts), not stage, agg_blocks, 12),
             out_shape=outs,
             in_specs=[pl.BlockSpec(memory_space=pl.ANY), HBM] + [VMEM] * (len(parts) + 1 + stage),
             out_specs=[VMEM] * len(outs),
@@ -265,7 +264,7 @@
                 pltpu.SMEM((agg_blocks, agg_blocks, count), jnp.int32),
                 pltpu.SemaphoreType.DMA,
                 pltpu.SemaphoreType.DMA,
-                pltpu.VMEM((1 + len(parts) * per_part, 2 * node, 2 * width), BF16),
+                pltpu.VMEM((1 + len(parts) * fan * per_part, 2 * node, 2 * width), BF16),
                 pltpu.VMEM((cols_total, KS_DEV * block[0], block[1]), F32),
             ]
             + [pltpu.VMEM((slot_count,) + block, F32)] * N_ACC,

time: 45.3 us -> 46.1 us (1.018)
  the two profiles are of different devices: /device:TPU:0 before, /device:TPU:26 now
where the time goes in v3:
time: 46.1 us; the launch traced here: 45.8 us
  waiting for transfers between devices  19.7 us (43%)
  Pallas kernels  14.1 us (31%)
  starting transfers between devices  10.3 us (22%)
  local copies, waits for them, and re-layouts  0.92 us (2%)
  other arithmetic  0.66 us (1%)
    ppermute x2, waiting for transfers between devices, on_device(): part = lax.ppermute(chip, ('row', 'col'), pairs)  10.9 us
    ppermute x6, waiting for transfers between devices, shift(): return lax.ppermute(x, 'col', [(i, to(i)) for i in range(cols_total)])  8.14 us
    pallas_call x2, Pallas kernels, on_device(): pl.pallas_call(partial(sum_kernel, len(parts), not stage, agg_blocks, 12)...  7.62 us
    ppermute x6, starting transfers between devices, shift(): return lax.ppermute(x, 'col', [(i, to(i)) for i in range(cols_total)])  5.58 us
    ppermute x2, starting transfers between devices, on_device(): part = lax.ppermute(chip, ('row', 'col'), pairs)  4.76 us
    pallas_call x1, Pallas kernels, on_device(): pl.pallas_call(partial(left_kernel, cols_total, fan, agg_blocks), out_sha...  4.62 us
    pallas_call x1, Pallas kernels, on_device(): pl.pallas_call(stage_kernel, out_shape=blocks, in_specs=[HBM], out_specs=...  1.9 us
  transfers between devices with their start and end apart: 11, of which 7 were waited for; matrix products, arithmetic and copies ran while one was open for 2% of the time, Pallas kernels for 22%

profile of v3, /device:TPU:26, one launch (start us, length us, event | category | flops | bytes accessed | tf_op | source)
XLA Modules:
  0.0 45.8 jit_solution(10040286817611038279)
XLA Ops:
  0.0 0.0 collective-permute-start.3
  0.0 0.9 %constant_dynamic-update-slice_fusion.1 = bf16[4,128,256]{2,1,0:T(8,128)(2,1)S(1)} fusion(bf16[2,128,256]{2,1,0:T(8,128)(2,1)} %piece_hbm.1), kind=kLoop, calls=%fused_computation.3 | loop fusion | bytes 262144
  0.9 0.6 %collective-permute-done.3 = bf16[2,128,256]{2,1,0:T(8,128)(2,1)S(1)} collective-permute-done((bf16[2,128,256]{2,1,0:T(8,128)(2,1)}, bf16[2,128,256]{2,1,0:T(8,128)(2,1)S(1)}, u32[]{:S(2)}, u32[]{:S(2)}) %collective-permute-start.3) | collective-permute-done | bytes 131104 | tf_op jit(solution)/shard_map/ppermute | solution.py:195
  1.6 1.2 %collective-permute-start.6 = (bf16[4,128,256]{2,1,0:T(8,128)(2,1)S(1)}, bf16[4,128,256]{2,1,0:T(8,128)(2,1)S(1)}, u32[]{:S(2)}, u32[]{:S(2)}) collective-permute-start(bf16[4,128,256]{2,1,0:T(8,128)(2,1)S(1)} %constant_dynamic-update-slice_fusion), channel_id=1, source_target_pairs={{0,8},{1,0},{2,24},{3,16},{4,28},{5,20},{6,12},{7,4},{8,9},{9,1},{... | collective-permute-start | bytes 786440 | tf_op jit(solution)/shard_map/ppermute | solution.py:210
  2.8 3.5 %collective-permute-start.4 = (bf16[4,128,256]{2,1,0:T(8,128)(2,1)S(1)}, bf16[4,128,256]{2,1,0:T(8,128)(2,1)S(1)}, u32[]{:S(2)}, u32[]{:S(2)}) collective-permute-start(bf16[4,128,256]{2,1,0:T(8,128)(2,1)S(1)} %constant_dynamic-update-slice_fusion), channel_id=1, source_target_pairs={{0,0},{1,8},{2,16},{3,24},{4,20},{5,28},{6,4},{7,12},{8,1},{9,9},{... | collective-permute-start | bytes 786440 | tf_op jit(solution)/shard_map/ppermute | solution.py:210
  6.3 10.9 %collective-permute-done.6.refs_0_ = bf16[4,128,256]{2,1,0:T(8,128)(2,1)S(1)} collective-permute-done((bf16[4,128,256]{2,1,0:T(8,128)(2,1)S(1)}, bf16[4,128,256]{2,1,0:T(8,128)(2,1)S(1)}, u32[]{:S(2)}, u32[]{:S(2)}) %collective-permute-start.6) | collective-permute-done | bytes 262176 | tf_op jit(solution)/shard_map/ppermute | solution.py:210
  17.2 0.0 collective-permute-start.7
  17.2 0.0 collective-permute-start
  17.2 0.0 collective-permute-start.1
  17.2 2.0 %collective-permute-start.2 = (bf16[2,128,256]{2,1,0:T(8,128)(2,1)}, bf16[2,128,256]{2,1,0:T(8,128)(2,1)S(1)}, u32[]{:S(2)}, u32[]{:S(2)}) collective-permute-start(bf16[2,128,256]{2,1,0:T(8,128)(2,1)} %piece_hbm.1), channel_id=1, source_target_pairs={{0,3},{1,0},{2,1},{3,2},{4,7},{5,4},{6,5},{7,6},{8,11},{9,8},{10,9... | collective-permute-start | bytes 393224 | tf_op jit(solution)/shard_map/ppermute | solution.py:191
  19.2 0.0 collective-permute-done.4.refs_0_
  19.3 0.0 collective-permute-start.5
  19.3 1.9 %stage.1.refs_3_ = bf16[96,128,128]{2,1,0:T(8,128)(2,1)S(1)} custom-call(bf16[96,128,128]{2,1,0:T(8,128)(2,1)} %bitcast.8), custom_call_target="tpu_custom_call" | custom-call | bytes 8388608 | tf_op jit(solution)/shard_map/stage/pallas_call | solution.py:217
  21.2 2.6 %collective-permute-done.refs_0_ = bf16[2,128,256]{2,1,0:T(8,128)(2,1)S(1)} collective-permute-done((bf16[2,128,256]{2,1,0:T(8,128)(2,1)}, bf16[2,128,256]{2,1,0:T(8,128)(2,1)S(1)}, u32[]{:S(2)}, u32[]{:S(2)}) %collective-permute-start) | collective-permute-done | bytes 131104 | tf_op jit(solution)/shard_map/ppermute | solution.py:191
  23.8 2.4 %collective-permute-done.1.refs_1_ = bf16[2,128,256]{2,1,0:T(8,128)(2,1)S(1)} collective-permute-done((bf16[2,128,256]{2,1,0:T(8,128)(2,1)}, bf16[2,128,256]{2,1,0:T(8,128)(2,1)S(1)}, u32[]{:S(2)}, u32[]{:S(2)}) %collective-permute-start.1) | collective-permute-done | bytes 131104 | tf_op jit(solution)/shard_map/ppermute | solution.py:191
  26.1 0.0 collective-permute-done.2.refs_2_
  26.2 4.6 %left.1 = (bf16[96,128,256]{2,1,0:T(8,128)(2,1)S(1)}, s32[98]{0:T(128)S(1)}) custom-call(s32[96]{0:T(128)} %bitcast.11, s32[96]{0:T(128)} %bitcast.12, bf16[2,128,256]{2,1,0:T(8,128)(2,1)} %piece_hbm.1, bf16[2,128,256]{2,1,0:T(8,128)(2,1)S(1)} %collective-permute-done.refs_0_, bf16[2,128,256]{2,1,0:T(8,128)(2,1)S(1)} %collective-permute-done.1.refs_1_, ...), custom_call_target="tpu_custom_call" | custom-call | flops 805306368 | bytes 10485760 | tf_op jit(solution)/shard_map/left/pallas_call | solution.py:227
  30.8 0.0 collective-permute-done.7.refs_1_
  30.8 3.3 %shard_map.55.refs_3_ = f32[32,32,128]{2,1,0:T(8,128)S(1)} custom-call(s32[98]{0:T(128)S(1)} %get-tuple-element.11.table_in, s32[4,4,96]{2,1,0:T(4,128)} %bitcast.9, bf16[4,128,256]{2,1,0:T(8,128)(2,1)S(1)} %collective-permute-done.6.refs_0_, bf16[4,128,256]{2,1,0:T(8,128)(2,1)S(1)} %collective-permute-done.7.refs_1_, ...), custom_call_target="tpu_custom_call" | custom-call | flops 1610612736 | bytes 10485760 | tf_op jit(solution)/shard_map/pallas_call | solution.py:257
  34.1 0.0 collective-permute-done.5.refs_1_
  34.2 4.3 %shard_map.56 = (f32[8,4096]{1,0:T(8,128)S(1)}, bf16[8,4096]{1,0:T(8,128)(2,1)S(1)}, bf16[8,4096]{1,0:T(8,128)(2,1)S(1)}, bf16[8,4096]{1,0:T(8,128)(2,1)S(1)}) custom-call(s32[98]{0:T(128)S(1)} %get-tuple-element.11.table_in, s32[4,4,96]{2,1,0:T(4,128)} %bitcast.10, bf16[4,128,256]{2,1,0:T(8,128)(2,1)S(1)} %collective-permute-done.4.refs_0_, ...), custom_call_target="tpu_custom_call" | custom-call | flops 1610612736 | bytes 10485760 | tf_op jit(solution)/shard_map/pallas_call | solution.py:257
  38.4 0.6 %collective-permute-start.10 = (bf16[8,4096]{1,0:T(8,128)(2,1)S(1)}, bf16[8,4096]{1,0:T(8,128)(2,1)S(1)}, u32[]{:S(2)}, u32[]{:S(2)}) collective-permute-start(bf16[8,4096]{1,0:T(8,128)(2,1)S(1)} %get-tuple-element.16), channel_id=1, source_target_pairs={{0,3},{1,2},{2,1},{3,0},{4,7},{5,6},{6,5},{7,4},{8,11},{9,10},{10,... | collective-permute-start | bytes 196616 | tf_op jit(solution)/shard_map/ppermute | solution.py:191
  39.1 1.7 %collective-permute-start.8 = (bf16[8,4096]{1,0:T(8,128)(2,1)S(1)}, bf16[8,4096]{1,0:T(8,128)(2,1)S(1)}, u32[]{:S(2)}, u32[]{:S(2)}) collective-permute-start(bf16[8,4096]{1,0:T(8,128)(2,1)S(1)} %get-tuple-element.14), channel_id=1, source_target_pairs={{0,1},{1,0},{2,3},{3,2},{4,5},{5,4},{6,7},{7,6},{8,9},{9,8},{10,11... | collective-permute-start | bytes 196616 | tf_op jit(solution)/shard_map/ppermute | solution.py:191
  40.8 1.2 %collective-permute-start.9 = (bf16[8,4096]{1,0:T(8,128)(2,1)S(1)}, bf16[8,4096]{1,0:T(8,128)(2,1)S(1)}, u32[]{:S(2)}, u32[]{:S(2)}) collective-permute-start(bf16[8,4096]{1,0:T(8,128)(2,1)S(1)} %get-tuple-element.15), channel_id=1, source_target_pairs={{0,2},{1,3},{2,0},{3,1},{4,6},{5,7},{6,4},{7,5},{8,10},{9,11},{10,... | collective-permute-start | bytes 196616 | tf_op jit(solution)/shard_map/ppermute | solution.py:191
  42.0 1.9 %collective-permute-done.10 = bf16[8,4096]{1,0:T(8,128)(2,1)S(1)} collective-permute-done((bf16[8,4096]{1,0:T(8,128)(2,1)S(1)}, bf16[8,4096]{1,0:T(8,128)(2,1)S(1)}, u32[]{:S(2)}, u32[]{:S(2)}) %collective-permute-start.10) | collective-permute-done | bytes 65568 | tf_op jit(solution)/shard_map/ppermute | solution.py:191
  43.8 0.6 %collective-permute-done.8 = bf16[8,4096]{1,0:T(8,128)(2,1)S(1)} collective-permute-done((bf16[8,4096]{1,0:T(8,128)(2,1)S(1)}, bf16[8,4096]{1,0:T(8,128)(2,1)S(1)}, u32[]{:S(2)}, u32[]{:S(2)}) %collective-permute-start.8) | collective-permute-done | bytes 65568 | tf_op jit(solution)/shard_map/ppermute | solution.py:191
  44.5 0.7 %collective-permute-done.9 = bf16[8,4096]{1,0:T(8,128)(2,1)S(1)} collective-permute-done((bf16[8,4096]{1,0:T(8,128)(2,1)S(1)}, bf16[8,4096]{1,0:T(8,128)(2,1)S(1)}, u32[]{:S(2)}, u32[]{:S(2)}) %collective-permute-start.9) | collective-permute-done | bytes 65568 | tf_op jit(solution)/shard_map/ppermute | solution.py:191
  45.1 0.7 %fusion = bf16[1,8,4096]{2,1,0:T(8,128)(2,1)} fusion(bf16[8,4096]{1,0:T(8,128)(2,1)S(1)} %collective-permute-done.10, bf16[8,4096]{1,0:T(8,128)(2,1)S(1)} %collective-permute-done.9, f32[8,4096]{1,0:T(8,128)S(1)} %get-tuple-element.13, bf16[8,4096]{1,0:T(8,128)(2,1)S(1)} %collective-permute-done.8), kind=kLoop, calls=%fused_computation.1 | loop fusion | flops 229376 | bytes 393216 | tf_op jit(solution)/shard_map/broadcast_in_dim | solution.py:279
  (1 shorter events, 0.0 us)
Async XLA Ops:
  0.0 1.6 %collective-permute-start.3 = (bf16[2,128,256]{2,1,0:T(8,128)(2,1)}, bf16[2,128,256]{2,1,0:T(8,128)(2,1)S(1)}, u32[]{:S(2)}, u32[]{:S(2)}) collective-permute-start(bf16[2,128,256]{2,1,0:T(8,128)(2,1)} %piece_hbm.1), channel_id=1, source_target_pairs={{0,4},{4,0},{8,12},{12,8},{16,20},{20,16},{24,28},{28,24},{1,5},{5... | collective-permute-start | bytes 393224 | tf_op jit(solution)/shard_map/ppermute | solution.py:195
  1.6 15.6 %collective-permute-start.6 = (bf16[4,128,256]{2,1,0:T(8,128)(2,1)S(1)}, bf16[4,128,256]{2,1,0:T(8,128)(2,1)S(1)}, u32[]{:S(2)}, u32[]{:S(2)}) collective-permute-start(bf16[4,128,256]{2,1,0:T(8,128)(2,1)S(1)} %constant_dynamic-update-slice_fusion), channel_id=1, source_target_pairs={{0,8},{1,0},{2,24},{3,16},{4,28},{5,20},{6,12},{7,4},{8,9},{9,1},{... | collective-permute-start | bytes 786440 | tf_op jit(solution)/shard_map/ppermute | solution.py:210
  2.8 16.4 %collective-permute-start.4 = (bf16[4,128,256]{2,1,0:T(8,128)(2,1)S(1)}, bf16[4,128,256]{2,1,0:T(8,128)(2,1)S(1)}, u32[]{:S(2)}, u32[]{:S(2)}) collective-permute-start(bf16[4,128,256]{2,1,0:T(8,128)(2,1)S(1)} %constant_dynamic-update-slice_fusion), channel_id=1, source_target_pairs={{0,0},{1,8},{2,16},{3,24},{4,20},{5,28},{6,4},{7,12},{8,1},{9,9},{... | collective-permute-start | bytes 786440 | tf_op jit(solution)/shard_map/ppermute | solution.py:210
  17.2 13.6 %collective-permute-start.7 = (bf16[4,128,256]{2,1,0:T(8,128)(2,1)S(1)}, bf16[4,128,256]{2,1,0:T(8,128)(2,1)S(1)}, u32[]{:S(2)}, u32[]{:S(2)}) collective-permute-start(bf16[4,128,256]{2,1,0:T(8,128)(2,1)S(1)} %collective-permute-done.6.refs_0_), channel_id=1, source_target_pairs={{0,4},{4,0},{8,12},{12,8},{16,20},{20,16},{24,28},{28,24},{1,5},{5... | collective-permute-start | bytes 786440 | tf_op jit(solution)/shard_map/ppermute | solution.py:195
  17.2 6.6 %collective-permute-start = (bf16[2,128,256]{2,1,0:T(8,128)(2,1)}, bf16[2,128,256]{2,1,0:T(8,128)(2,1)S(1)}, u32[]{:S(2)}, u32[]{:S(2)}) collective-permute-start(bf16[2,128,256]{2,1,0:T(8,128)(2,1)} %piece_hbm.1), channel_id=1, source_target_pairs={{0,1},{1,2},{2,3},{3,0},{4,5},{5,6},{6,7},{7,4},{8,9},{9,10},{10,1... | collective-permute-start | bytes 393224 | tf_op jit(solution)/shard_map/ppermute | solution.py:191
  17.2 8.9 %collective-permute-start.1 = (bf16[2,128,256]{2,1,0:T(8,128)(2,1)}, bf16[2,128,256]{2,1,0:T(8,128)(2,1)S(1)}, u32[]{:S(2)}, u32[]{:S(2)}) collective-permute-start(bf16[2,128,256]{2,1,0:T(8,128)(2,1)} %piece_hbm.1), channel_id=1, source_target_pairs={{0,2},{1,3},{2,0},{3,1},{4,6},{5,7},{6,4},{7,5},{8,10},{9,11},{10,... | collective-permute-start | bytes 393224 | tf_op jit(solution)/shard_map/ppermute | solution.py:191
  17.2 8.9 %collective-permute-start.2 = (bf16[2,128,256]{2,1,0:T(8,128)(2,1)}, bf16[2,128,256]{2,1,0:T(8,128)(2,1)S(1)}, u32[]{:S(2)}, u32[]{:S(2)}) collective-permute-start(bf16[2,128,256]{2,1,0:T(8,128)(2,1)} %piece_hbm.1), channel_id=1, source_target_pairs={{0,3},{1,0},{2,1},{3,2},{4,7},{5,4},{6,5},{7,6},{8,11},{9,8},{10,9... | collective-permute-start | bytes 393224 | tf_op jit(solution)/shard_map/ppermute | solution.py:191
  19.3 14.9 %collective-permute-start.5 = (bf16[4,128,256]{2,1,0:T(8,128)(2,1)S(1)}, bf16[4,128,256]{2,1,0:T(8,128)(2,1)S(1)}, u32[]{:S(2)}, u32[]{:S(2)}) collective-permute-start(bf16[4,128,256]{2,1,0:T(8,128)(2,1)S(1)} %collective-permute-done.4.refs_0_), channel_id=1, source_target_pairs={{0,4},{4,0},{8,12},{12,8},{16,20},{20,16},{24,28},{28,24},{1,5},{5... | collective-permute-start | bytes 786440 | tf_op jit(solution)/shard_map/ppermute | solution.py:195
  38.4 5.4 %collective-permute-start.10 = (bf16[8,4096]{1,0:T(8,128)(2,1)S(1)}, bf16[8,4096]{1,0:T(8,128)(2,1)S(1)}, u32[]{:S(2)}, u32[]{:S(2)}) collective-permute-start(bf16[8,4096]{1,0:T(8,128)(2,1)S(1)} %get-tuple-element.16), channel_id=1, source_target_pairs={{0,3},{1,2},{2,1},{3,0},{4,7},{5,6},{6,5},{7,4},{8,11},{9,10},{10,... | collective-permute-start | bytes 196616 | tf_op jit(solution)/shard_map/ppermute | solution.py:191
  39.1 5.4 %collective-permute-start.8 = (bf16[8,4096]{1,0:T(8,128)(2,1)S(1)}, bf16[8,4096]{1,0:T(8,128)(2,1)S(1)}, u32[]{:S(2)}, u32[]{:S(2)}) collective-permute-start(bf16[8,4096]{1,0:T(8,128)(2,1)S(1)} %get-tuple-element.14), channel_id=1, source_target_pairs={{0,1},{1,0},{2,3},{3,2},{4,5},{5,4},{6,7},{7,6},{8,9},{9,8},{10,11... | collective-permute-start | bytes 196616 | tf_op jit(solution)/shard_map/ppermute | solution.py:191
  40.8 4.3 %collective-permute-start.9 = (bf16[8,4096]{1,0:T(8,128)(2,1)S(1)}, bf16[8,4096]{1,0:T(8,128)(2,1)S(1)}, u32[]{:S(2)}, u32[]{:S(2)}) collective-permute-start(bf16[8,4096]{1,0:T(8,128)(2,1)S(1)} %get-tuple-element.15), channel_id=1, source_target_pairs={{0,2},{1,3},{2,0},{3,1},{4,6},{5,7},{6,4},{7,5},{8,10},{9,11},{10,... | collective-permute-start | bytes 196616 | tf_op jit(solution)/shard_map/ppermute | solution.py:191

commit v4 on v3

--- a/solution.py
+++ b/solution.py
@@ -111,7 +111,7 @@
     top, bottom = [], []
     for v in range(agg_blocks // 2):
         straight = piece[:, v * 2 * agg : (v + 1) * 2 * agg]
-        turned = pltpu.roll(straight.astype(F32), agg, 1).astype(BF16)
+        turned = pltpu.roll(straight, agg, 1)
         top += [jnp.where(low, straight, zero), jnp.where(low, turned, zero)]
         bottom += [jnp.where(low, zero, turned), jnp.where(low, zero, straight)]
     return top, bottom
@@ -122,9 +122,9 @@
     before = None
     if not early:
         before, rest = rest[0], rest[1:]
-    outs, rest = rest[: -6 - N_ACC], rest[-6 - N_ACC :]
-    table_ref, slots_ref, table_sem, slot_sem, wide, turn = rest[:6]
-    accs = rest[6:]
+    outs, rest = rest[: -5 - N_ACC], rest[-5 - N_ACC :]
+    table_ref, slots_ref, table_sem, slot_sem, wide = rest[:5]
+    accs = rest[5:]
     count = left_ref.shape[0]
     get_slots = pltpu.make_async_copy(slots_hbm, slots_ref, slot_sem)
     get_slots.start()
@@ -173,9 +173,9 @@
         total = accs[0][slots]
         for acc in accs[1:]:
             total += acc[slots]
-        turn[step] = total.reshape(KS_DEV * half, lanes)
+        across_slots = jnp.swapaxes(total, 0, 1)
         for a in range(half):
-            out[:, a * lanes : (a + 1) * lanes] = turn[step, pl.ds(a, KS_DEV, stride=half), :].astype(out.dtype)
+            out[:, a * lanes : (a + 1) * lanes] = across_slots[a].astype(out.dtype)
 
 
 def on_device(a_blocks, a_rows, a_cols, p_blocks, coarse_slot):
@@ -265,7 +265,6 @@
                 pltpu.SemaphoreType.DMA,
                 pltpu.SemaphoreType.DMA,
                 pltpu.VMEM((1 + len(parts) * fan * per_part, 2 * node, 2 * width), BF16),
-                pltpu.VMEM((cols_total, KS_DEV * block[0], block[1]), F32),
             ]
             + [pltpu.VMEM((slot_count,) + block, F32)] * N_ACC,
             compiler_params=pltpu.CompilerParams(vmem_limit_bytes=36 << 20),

time: 46.1 us -> 45.9 us (level)
  no operation moved by 1% of the time
where the time goes in v4:
time: 45.9 us; the launch traced here: 45.6 us
  waiting for transfers between devices  19.7 us (43%)
  Pallas kernels  13.9 us (30%)
  starting transfers between devices  10.3 us (22%)
  local copies, waits for them, and re-layouts  0.92 us (2%)
  other arithmetic  0.66 us (1%)
    ppermute x2, waiting for transfers between devices, on_device(): part = lax.ppermute(chip, ('row', 'col'), pairs)  10.9 us
    ppermute x6, waiting for transfers between devices, shift(): return lax.ppermute(x, 'col', [(i, to(i)) for i in range(cols_total)])  8.15 us
    pallas_call x2, Pallas kernels, on_device(): pl.pallas_call(partial(sum_kernel, len(parts), not stage, agg_blocks, 12)...  7.4 us
    ppermute x6, starting transfers between devices, shift(): return lax.ppermute(x, 'col', [(i, to(i)) for i in range(cols_total)])  5.58 us
    ppermute x2, starting transfers between devices, on_device(): part = lax.ppermute(chip, ('row', 'col'), pairs)  4.76 us
    pallas_call x1, Pallas kernels, on_device(): pl.pallas_call(partial(left_kernel, cols_total, fan, agg_blocks), out_sha...  4.62 us
    pallas_call x1, Pallas kernels, on_device(): pl.pallas_call(stage_kernel, out_shape=blocks, in_specs=[HBM], out_specs=...  1.9 us
  transfers between devices with their start and end apart: 11, of which 7 were waited for; matrix products, arithmetic and copies ran while one was open for 2% of the time, Pallas kernels for 22%

profile of v4, /device:TPU:26, one launch (start us, length us, event | category | flops | bytes accessed | tf_op | source)
XLA Modules:
  0.0 45.6 jit_solution(11667616698490786840)
XLA Ops:
  0.0 0.0 collective-permute-start.3
  0.0 0.9 %constant_dynamic-update-slice_fusion.1 = bf16[4,128,256]{2,1,0:T(8,128)(2,1)S(1)} fusion(bf16[2,128,256]{2,1,0:T(8,128)(2,1)} %piece_hbm.1), kind=kLoop, calls=%fused_computation.3 | loop fusion | bytes 262144
  0.9 0.6 %collective-permute-done.3 = bf16[2,128,256]{2,1,0:T(8,128)(2,1)S(1)} collective-permute-done((bf16[2,128,256]{2,1,0:T(8,128)(2,1)}, bf16[2,128,256]{2,1,0:T(8,128)(2,1)S(1)}, u32[]{:S(2)}, u32[]{:S(2)}) %collective-permute-start.3) | collective-permute-done | bytes 131104 | tf_op jit(solution)/shard_map/ppermute | solution.py:195
  1.6 1.2 %collective-permute-start.6 = (bf16[4,128,256]{2,1,0:T(8,128)(2,1)S(1)}, bf16[4,128,256]{2,1,0:T(8,128)(2,1)S(1)}, u32[]{:S(2)}, u32[]{:S(2)}) collective-permute-start(bf16[4,128,256]{2,1,0:T(8,128)(2,1)S(1)} %constant_dynamic-update-slice_fusion), channel_id=1, source_target_pairs={{0,8},{1,0},{2,24},{3,16},{4,28},{5,20},{6,12},{7,4},{8,9},{9,1},{... | collective-permute-start | bytes 786440 | tf_op jit(solution)/shard_map/ppermute | solution.py:210
  2.8 3.5 %collective-permute-start.4 = (bf16[4,128,256]{2,1,0:T(8,128)(2,1)S(1)}, bf16[4,128,256]{2,1,0:T(8,128)(2,1)S(1)}, u32[]{:S(2)}, u32[]{:S(2)}) collective-permute-start(bf16[4,128,256]{2,1,0:T(8,128)(2,1)S(1)} %constant_dynamic-update-slice_fusion), channel_id=1, source_target_pairs={{0,0},{1,8},{2,16},{3,24},{4,20},{5,28},{6,4},{7,12},{8,1},{9,9},{... | collective-permute-start | bytes 786440 | tf_op jit(solution)/shard_map/ppermute | solution.py:210
  6.3 10.9 %collective-permute-done.6.refs_0_ = bf16[4,128,256]{2,1,0:T(8,128)(2,1)S(1)} collective-permute-done((bf16[4,128,256]{2,1,0:T(8,128)(2,1)S(1)}, bf16[4,128,256]{2,1,0:T(8,128)(2,1)S(1)}, u32[]{:S(2)}, u32[]{:S(2)}) %collective-permute-start.6) | collective-permute-done | bytes 262176 | tf_op jit(solution)/shard_map/ppermute | solution.py:210
  17.2 0.0 collective-permute-start.7
  17.2 0.0 collective-permute-start
  17.2 0.0 collective-permute-start.1
  17.2 2.0 %collective-permute-start.2 = (bf16[2,128,256]{2,1,0:T(8,128)(2,1)}, bf16[2,128,256]{2,1,0:T(8,128)(2,1)S(1)}, u32[]{:S(2)}, u32[]{:S(2)}) collective-permute-start(bf16[2,128,256]{2,1,0:T(8,128)(2,1)} %piece_hbm.1), channel_id=1, source_target_pairs={{0,3},{1,0},{2,1},{3,2},{4,7},{5,4},{6,5},{7,6},{8,11},{9,8},{10,9... | collective-permute-start | bytes 393224 | tf_op jit(solution)/shard_map/ppermute | solution.py:191
  19.2 0.0 collective-permute-done.4.refs_0_
  19.3 0.0 collective-permute-start.5
  19.3 1.9 %stage.1.refs_3_ = bf16[96,128,128]{2,1,0:T(8,128)(2,1)S(1)} custom-call(bf16[96,128,128]{2,1,0:T(8,128)(2,1)} %bitcast.8), custom_call_target="tpu_custom_call" | custom-call | bytes 8388608 | tf_op jit(solution)/shard_map/stage/pallas_call | solution.py:217
  21.2 2.6 %collective-permute-done.refs_0_ = bf16[2,128,256]{2,1,0:T(8,128)(2,1)S(1)} collective-permute-done((bf16[2,128,256]{2,1,0:T(8,128)(2,1)}, bf16[2,128,256]{2,1,0:T(8,128)(2,1)S(1)}, u32[]{:S(2)}, u32[]{:S(2)}) %collective-permute-start) | collective-permute-done | bytes 131104 | tf_op jit(solution)/shard_map/ppermute | solution.py:191
  23.8 2.4 %collective-permute-done.1.refs_1_ = bf16[2,128,256]{2,1,0:T(8,128)(2,1)S(1)} collective-permute-done((bf16[2,128,256]{2,1,0:T(8,128)(2,1)}, bf16[2,128,256]{2,1,0:T(8,128)(2,1)S(1)}, u32[]{:S(2)}, u32[]{:S(2)}) %collective-permute-start.1) | collective-permute-done | bytes 131104 | tf_op jit(solution)/shard_map/ppermute | solution.py:191
  26.1 0.0 collective-permute-done.2.refs_2_
  26.2 4.6 %left.1 = (bf16[96,128,256]{2,1,0:T(8,128)(2,1)S(1)}, s32[98]{0:T(128)S(1)}) custom-call(s32[96]{0:T(128)} %bitcast.11, s32[96]{0:T(128)} %bitcast.12, bf16[2,128,256]{2,1,0:T(8,128)(2,1)} %piece_hbm.1, bf16[2,128,256]{2,1,0:T(8,128)(2,1)S(1)} %collective-permute-done.refs_0_, bf16[2,128,256]{2,1,0:T(8,128)(2,1)S(1)} %collective-permute-done.1.refs_1_, ...), custom_call_target="tpu_custom_call" | custom-call | flops 805306368 | bytes 10485760 | tf_op jit(solution)/shard_map/left/pallas_call | solution.py:227
  30.8 0.0 collective-permute-done.7.refs_1_
  30.8 3.3 %shard_map.55.refs_3_ = f32[32,32,128]{2,1,0:T(8,128)S(1)} custom-call(s32[98]{0:T(128)S(1)} %get-tuple-element.11.table_in, s32[4,4,96]{2,1,0:T(4,128)} %bitcast.9, bf16[4,128,256]{2,1,0:T(8,128)(2,1)S(1)} %collective-permute-done.6.refs_0_, bf16[4,128,256]{2,1,0:T(8,128)(2,1)S(1)} %collective-permute-done.7.refs_1_, ...), custom_call_target="tpu_custom_call" | custom-call | flops 1610612736 | bytes 10485760 | tf_op jit(solution)/shard_map/pallas_call | solution.py:257
  34.1 0.0 collective-permute-done.5.refs_1_
  34.2 4.1 %shard_map.56 = (f32[8,4096]{1,0:T(8,128)S(1)}, bf16[8,4096]{1,0:T(8,128)(2,1)S(1)}, bf16[8,4096]{1,0:T(8,128)(2,1)S(1)}, bf16[8,4096]{1,0:T(8,128)(2,1)S(1)}) custom-call(s32[98]{0:T(128)S(1)} %get-tuple-element.11.table_in, s32[4,4,96]{2,1,0:T(4,128)} %bitcast.10, bf16[4,128,256]{2,1,0:T(8,128)(2,1)S(1)} %collective-permute-done.4.refs_0_, ...), custom_call_target="tpu_custom_call" | custom-call | flops 1610612736 | bytes 10485760 | tf_op jit(solution)/shard_map/pallas_call | solution.py:257
  38.2 0.6 %collective-permute-start.10 = (bf16[8,4096]{1,0:T(8,128)(2,1)S(1)}, bf16[8,4096]{1,0:T(8,128)(2,1)S(1)}, u32[]{:S(2)}, u32[]{:S(2)}) collective-permute-start(bf16[8,4096]{1,0:T(8,128)(2,1)S(1)} %get-tuple-element.16), channel_id=1, source_target_pairs={{0,3},{1,2},{2,1},{3,0},{4,7},{5,6},{6,5},{7,4},{8,11},{9,10},{10,... | collective-permute-start | bytes 196616 | tf_op jit(solution)/shard_map/ppermute | solution.py:191
  38.9 1.7 %collective-permute-start.8 = (bf16[8,4096]{1,0:T(8,128)(2,1)S(1)}, bf16[8,4096]{1,0:T(8,128)(2,1)S(1)}, u32[]{:S(2)}, u32[]{:S(2)}) collective-permute-start(bf16[8,4096]{1,0:T(8,128)(2,1)S(1)} %get-tuple-element.14), channel_id=1, source_target_pairs={{0,1},{1,0},{2,3},{3,2},{4,5},{5,4},{6,7},{7,6},{8,9},{9,8},{10,11... | collective-permute-start | bytes 196616 | tf_op jit(solution)/shard_map/ppermute | solution.py:191
  40.6 1.2 %collective-permute-start.9 = (bf16[8,4096]{1,0:T(8,128)(2,1)S(1)}, bf16[8,4096]{1,0:T(8,128)(2,1)S(1)}, u32[]{:S(2)}, u32[]{:S(2)}) collective-permute-start(bf16[8,4096]{1,0:T(8,128)(2,1)S(1)} %get-tuple-element.15), channel_id=1, source_target_pairs={{0,2},{1,3},{2,0},{3,1},{4,6},{5,7},{6,4},{7,5},{8,10},{9,11},{10,... | collective-permute-start | bytes 196616 | tf_op jit(solution)/shard_map/ppermute | solution.py:191
  41.8 1.9 %collective-permute-done.10 = bf16[8,4096]{1,0:T(8,128)(2,1)S(1)} collective-permute-done((bf16[8,4096]{1,0:T(8,128)(2,1)S(1)}, bf16[8,4096]{1,0:T(8,128)(2,1)S(1)}, u32[]{:S(2)}, u32[]{:S(2)}) %collective-permute-start.10) | collective-permute-done | bytes 65568 | tf_op jit(solution)/shard_map/ppermute | solution.py:191
  43.6 0.6 %collective-permute-done.8 = bf16[8,4096]{1,0:T(8,128)(2,1)S(1)} collective-permute-done((bf16[8,4096]{1,0:T(8,128)(2,1)S(1)}, bf16[8,4096]{1,0:T(8,128)(2,1)S(1)}, u32[]{:S(2)}, u32[]{:S(2)}) %collective-permute-start.8) | collective-permute-done | bytes 65568 | tf_op jit(solution)/shard_map/ppermute | solution.py:191
  44.2 0.7 %collective-permute-done.9 = bf16[8,4096]{1,0:T(8,128)(2,1)S(1)} collective-permute-done((bf16[8,4096]{1,0:T(8,128)(2,1)S(1)}, bf16[8,4096]{1,0:T(8,128)(2,1)S(1)}, u32[]{:S(2)}, u32[]{:S(2)}) %collective-permute-start.9) | collective-permute-done | bytes 65568 | tf_op jit(solution)/shard_map/ppermute | solution.py:191
  44.9 0.7 %fusion = bf16[1,8,4096]{2,1,0:T(8,128)(2,1)} fusion(bf16[8,4096]{1,0:T(8,128)(2,1)S(1)} %collective-permute-done.10, bf16[8,4096]{1,0:T(8,128)(2,1)S(1)} %collective-permute-done.9, f32[8,4096]{1,0:T(8,128)S(1)} %get-tuple-element.13, bf16[8,4096]{1,0:T(8,128)(2,1)S(1)} %collective-permute-done.8), kind=kLoop, calls=%fused_computation.1 | loop fusion | flops 229376 | bytes 393216 | tf_op jit(solution)/shard_map/broadcast_in_dim | solution.py:278
  (1 shorter events, 0.0 us)
Async XLA Ops:
  0.0 1.6 %collective-permute-start.3 = (bf16[2,128,256]{2,1,0:T(8,128)(2,1)}, bf16[2,128,256]{2,1,0:T(8,128)(2,1)S(1)}, u32[]{:S(2)}, u32[]{:S(2)}) collective-permute-start(bf16[2,128,256]{2,1,0:T(8,128)(2,1)} %piece_hbm.1), channel_id=1, source_target_pairs={{0,4},{4,0},{8,12},{12,8},{16,20},{20,16},{24,28},{28,24},{1,5},{5... | collective-permute-start | bytes 393224 | tf_op jit(solution)/shard_map/ppermute | solution.py:195
  1.6 15.6 %collective-permute-start.6 = (bf16[4,128,256]{2,1,0:T(8,128)(2,1)S(1)}, bf16[4,128,256]{2,1,0:T(8,128)(2,1)S(1)}, u32[]{:S(2)}, u32[]{:S(2)}) collective-permute-start(bf16[4,128,256]{2,1,0:T(8,128)(2,1)S(1)} %constant_dynamic-update-slice_fusion), channel_id=1, source_target_pairs={{0,8},{1,0},{2,24},{3,16},{4,28},{5,20},{6,12},{7,4},{8,9},{9,1},{... | collective-permute-start | bytes 786440 | tf_op jit(solution)/shard_map/ppermute | solution.py:210
  2.8 16.4 %collective-permute-start.4 = (bf16[4,128,256]{2,1,0:T(8,128)(2,1)S(1)}, bf16[4,128,256]{2,1,0:T(8,128)(2,1)S(1)}, u32[]{:S(2)}, u32[]{:S(2)}) collective-permute-start(bf16[4,128,256]{2,1,0:T(8,128)(2,1)S(1)} %constant_dynamic-update-slice_fusion), channel_id=1, source_target_pairs={{0,0},{1,8},{2,16},{3,24},{4,20},{5,28},{6,4},{7,12},{8,1},{9,9},{... | collective-permute-start | bytes 786440 | tf_op jit(solution)/shard_map/ppermute | solution.py:210
  17.2 13.6 %collective-permute-start.7 = (bf16[4,128,256]{2,1,0:T(8,128)(2,1)S(1)}, bf16[4,128,256]{2,1,0:T(8,128)(2,1)S(1)}, u32[]{:S(2)}, u32[]{:S(2)}) collective-permute-start(bf16[4,128,256]{2,1,0:T(8,128)(2,1)S(1)} %collective-permute-done.6.refs_0_), channel_id=1, source_target_pairs={{0,4},{4,0},{8,12},{12,8},{16,20},{20,16},{24,28},{28,24},{1,5},{5... | collective-permute-start | bytes 786440 | tf_op jit(solution)/shard_map/ppermute | solution.py:195
  17.2 6.6 %collective-permute-start = (bf16[2,128,256]{2,1,0:T(8,128)(2,1)}, bf16[2,128,256]{2,1,0:T(8,128)(2,1)S(1)}, u32[]{:S(2)}, u32[]{:S(2)}) collective-permute-start(bf16[2,128,256]{2,1,0:T(8,128)(2,1)} %piece_hbm.1), channel_id=1, source_target_pairs={{0,1},{1,2},{2,3},{3,0},{4,5},{5,6},{6,7},{7,4},{8,9},{9,10},{10,1... | collective-permute-start | bytes 393224 | tf_op jit(solution)/shard_map/ppermute | solution.py:191
  17.2 8.9 %collective-permute-start.1 = (bf16[2,128,256]{2,1,0:T(8,128)(2,1)}, bf16[2,128,256]{2,1,0:T(8,128)(2,1)S(1)}, u32[]{:S(2)}, u32[]{:S(2)}) collective-permute-start(bf16[2,128,256]{2,1,0:T(8,128)(2,1)} %piece_hbm.1), channel_id=1, source_target_pairs={{0,2},{1,3},{2,0},{3,1},{4,6},{5,7},{6,4},{7,5},{8,10},{9,11},{10,... | collective-permute-start | bytes 393224 | tf_op jit(solution)/shard_map/ppermute | solution.py:191
  17.2 8.9 %collective-permute-start.2 = (bf16[2,128,256]{2,1,0:T(8,128)(2,1)}, bf16[2,128,256]{2,1,0:T(8,128)(2,1)S(1)}, u32[]{:S(2)}, u32[]{:S(2)}) collective-permute-start(bf16[2,128,256]{2,1,0:T(8,128)(2,1)} %piece_hbm.1), channel_id=1, source_target_pairs={{0,3},{1,0},{2,1},{3,2},{4,7},{5,4},{6,5},{7,6},{8,11},{9,8},{10,9... | collective-permute-start | bytes 393224 | tf_op jit(solution)/shard_map/ppermute | solution.py:191
  19.3 14.9 %collective-permute-start.5 = (bf16[4,128,256]{2,1,0:T(8,128)(2,1)S(1)}, bf16[4,128,256]{2,1,0:T(8,128)(2,1)S(1)}, u32[]{:S(2)}, u32[]{:S(2)}) collective-permute-start(bf16[4,128,256]{2,1,0:T(8,128)(2,1)S(1)} %collective-permute-done.4.refs_0_), channel_id=1, source_target_pairs={{0,4},{4,0},{8,12},{12,8},{16,20},{20,16},{24,28},{28,24},{1,5},{5... | collective-permute-start | bytes 786440 | tf_op jit(solution)/shard_map/ppermute | solution.py:195
  38.2 5.4 %collective-permute-start.10 = (bf16[8,4096]{1,0:T(8,128)(2,1)S(1)}, bf16[8,4096]{1,0:T(8,128)(2,1)S(1)}, u32[]{:S(2)}, u32[]{:S(2)}) collective-permute-start(bf16[8,4096]{1,0:T(8,128)(2,1)S(1)} %get-tuple-element.16), channel_id=1, source_target_pairs={{0,3},{1,2},{2,1},{3,0},{4,7},{5,6},{6,5},{7,4},{8,11},{9,10},{10,... | collective-permute-start | bytes 196616 | tf_op jit(solution)/shard_map/ppermute | solution.py:191
  38.9 5.4 %collective-permute-start.8 = (bf16[8,4096]{1,0:T(8,128)(2,1)S(1)}, bf16[8,4096]{1,0:T(8,128)(2,1)S(1)}, u32[]{:S(2)}, u32[]{:S(2)}) collective-permute-start(bf16[8,4096]{1,0:T(8,128)(2,1)S(1)} %get-tuple-element.14), channel_id=1, source_target_pairs={{0,1},{1,0},{2,3},{3,2},{4,5},{5,4},{6,7},{7,6},{8,9},{9,8},{10,11... | collective-permute-start | bytes 196616 | tf_op jit(solution)/shard_map/ppermute | solution.py:191
  40.6 4.3 %collective-permute-start.9 = (bf16[8,4096]{1,0:T(8,128)(2,1)S(1)}, bf16[8,4096]{1,0:T(8,128)(2,1)S(1)}, u32[]{:S(2)}, u32[]{:S(2)}) collective-permute-start(bf16[8,4096]{1,0:T(8,128)(2,1)S(1)} %get-tuple-element.15), channel_id=1, source_target_pairs={{0,2},{1,3},{2,0},{3,1},{4,6},{5,7},{6,4},{7,5},{8,10},{9,11},{10,... | collective-permute-start | bytes 196616 | tf_op jit(solution)/shard_map/ppermute | solution.py:191
